TPU v7x, 32 devices: a whole 2x2x4 slice. The times are simulated.
32 devices in a mesh: req: 2 (over y), ep: 16 (over z, x, core).
Axes of the slice: x: 2, y: 2, z: 4, core: 2. Of those that a mesh axis runs over, the one named last changes fastest.
Arguments:
- queries: bfloat16 [256, 64, 576], P(('req', 'ep')), may hold values from -7 to 7
- latent_cache: bfloat16 [32, 512, 576], P(('req', 'ep')), may hold values from -3 to 3
- new_latents: bfloat16 [256, 576], P(('req', 'ep')), may hold values from -4 to 4
- parents: int32 [16, 16], replicated, may hold values from 0 to 14, as said below
- cache_len: int32 [16], replicated, may hold values from 128 to 1024
- tokens: bfloat16 [256, 7168], P(('req', 'ep')), may hold values from -6 to 6
- route_ids: int32 [256, 8], P(('req', 'ep')), may hold values from 0 to 15, all different within a row; in each aligned block of 8 rows (0 to 7, 8 to 15, ...) at most 5 rows name the same one
- route_scores: float32 [256, 8], P(('req', 'ep')), may hold values from 0.05 to 1
- w_gate: bfloat16 [16, 7168, 2048], P('ep', None, 'req'), may hold values from -0.0625 to 0.0625
- w_up: bfloat16 [16, 7168, 2048], P('ep', None, 'req'), may hold values from -0.0625 to 0.0625
- w_down: bfloat16 [16, 2048, 7168], P('ep', 'req'), may hold values from -0.125 to 0.125
Outputs:
- attention_out: bfloat16 [256, 64, 512], P(('req', 'ep'))
- moe_out: bfloat16 [256, 7168], P(('req', 'ep'))
Inputs may be any that keep to these rules, and one draw needn't show every extreme that they name: `route_ids`: each row names 8 different experts. Among the 8 tokens of one device (aligned blocks of 8 rows) no expert is named by more than 5 tokens, a bound that some block reaches. parents[q, 0] = 0 and parents[q, j] < j for j >= 1.
All inputs are finite; a program needn't handle non-finite values.
Results may differ from a plain program's by a relative error of at most 0.015.
Values may be sent and summed in bfloat16 or wider, within the bound.
No kernel may reach another device: no remote copies, remote signals or barrier semaphores. Data moves between devices by JAX's collectives and lax.ppermute only.
A program may use at most 128 MiB of HBM per device.

v0:
```python
import jax
import jax.numpy as jnp
from jax import lax
from jax.sharding import PartitionSpec as P

VDIM = 512


score_scale = 192.0 ** (-0.5)
route_scale = 2.5


def partner(block, axis, stride):
    count = lax.axis_size(axis)
    route = []
    for low in range(count):
        high = low | 1 << stride
        if high != low and high < count:
            route += [(low, high), (high, low)]
    return lax.ppermute(block, axis, route)


def ancestor_table(parent_row):
    node_count = parent_row.shape[0]
    node_ids = jnp.arange(node_count, dtype=jnp.int32)
    current = node_ids
    visible = node_ids[:, None] == node_ids[None, :]
    for repeat in range(node_count):
        current = parent_row[current]
        visible = visible | (current[:, None] == node_ids[None, :])
    return visible


def expert_mlp(row_block, w_gate, w_up, w_down):
    gate_val = jnp.dot(row_block, w_gate[0], preferred_element_type=jnp.float32)
    up_val = jnp.dot(row_block, w_up[0], preferred_element_type=jnp.float32)
    hidden = (jax.nn.silu(gate_val) * up_val).astype(jnp.bfloat16)
    return jnp.dot(hidden, w_down[0], preferred_element_type=jnp.float32).astype(jnp.bfloat16)


def body(
    queries,
    latent_cache,
    new_latents,
    parents,
    cache_len,
    tokens,
    route_ids,
    route_scores,
    w_gate,
    w_up,
    w_down,
):
    ep_count = lax.axis_size("ep")
    position = lax.axis_index("req") * ep_count + lax.axis_index("ep")
    request = position // 2
    half_index = position % 2
    tok_dev = tokens.shape[0]
    model_width = tokens.shape[1]
    other_cache, other_fresh = partner((latent_cache, new_latents), "ep", 0)
    lower_half = half_index == 0
    cache_rows = jnp.concatenate(
        [
            jnp.where(lower_half, latent_cache[0], other_cache[0]),
            jnp.where(lower_half, other_cache[0], latent_cache[0]),
        ],
        axis=0,
    )
    fresh_rows = jnp.concatenate(
        [
            jnp.where(lower_half, new_latents, other_fresh),
            jnp.where(lower_half, other_fresh, new_latents),
        ],
        axis=0,
    )
    key_rows = jnp.concatenate([cache_rows, fresh_rows], axis=0)
    context = cache_rows.shape[0]
    parent_row = lax.dynamic_index_in_dim(parents, request, 0, keepdims=False)
    tree_vis = lax.dynamic_slice_in_dim(
        ancestor_table(parent_row), half_index * tok_dev, tok_dev, 0
    )
    length = lax.dynamic_index_in_dim(cache_len, request, 0, keepdims=False)
    cached = jnp.arange(context, dtype=jnp.int32) < length
    visible = jnp.concatenate(
        [jnp.broadcast_to(cached[None, :], (tok_dev, context)), tree_vis], axis=1
    )
    head_count = queries.shape[1]
    flat_query = queries.reshape(tok_dev * head_count, queries.shape[2])
    scores = (
        lax.dot_general(
            flat_query, key_rows, (((1,), (1,)), ((), ())), preferred_element_type=jnp.float32
        )
        * score_scale
    )
    scores = scores.reshape(tok_dev, head_count, key_rows.shape[0])
    masked = jnp.where(visible[:, None, :], scores, -jnp.inf)
    row_max = jnp.max(masked, axis=-1, keepdims=True)
    shifted = jnp.exp(masked - row_max)
    attn_probs = (shifted / jnp.sum(shifted, axis=-1, keepdims=True)).astype(jnp.bfloat16)
    value_rows = key_rows[:, :VDIM]
    attended = jnp.dot(
        attn_probs.reshape(tok_dev * head_count, key_rows.shape[0]),
        value_rows,
        preferred_element_type=jnp.float32,
    )
    attention_out = attended.reshape(tok_dev, head_count, VDIM).astype(jnp.bfloat16)
    top_count = route_ids.shape[1]
    capacity = min(tok_dev, tok_dev * top_count // ep_count + 1)
    route_weight = route_scale * route_scores / jnp.sum(route_scores, axis=1, keepdims=True)
    pair_ids = route_ids.reshape(-1)
    onehot = (pair_ids[:, None] == jnp.arange(ep_count, dtype=jnp.int32)[None, :]).astype(jnp.int32)
    slot_rank = jnp.sum(jnp.cumsum(onehot, axis=0) * onehot, axis=1) - 1
    slot_of = (pair_ids * capacity + slot_rank).reshape(tok_dev, top_count)
    slot_ids = jnp.arange(ep_count * capacity, dtype=jnp.int32)
    slot_hits = slot_of[None, :, :] == slot_ids[:, None, None]
    dispatch = jnp.any(slot_hits, axis=2).astype(jnp.bfloat16)
    combine = jnp.sum(jnp.where(slot_hits, route_weight[None, :, :], 0.0), axis=2)
    outgoing = jnp.dot(dispatch, tokens, preferred_element_type=jnp.float32).astype(jnp.bfloat16)
    outgoing = outgoing.reshape(ep_count, capacity, model_width)
    arrived = lax.all_to_all(outgoing, "ep", split_axis=0, concat_axis=0, tiled=True)
    partial_value = expert_mlp(
        lax.all_gather(
            arrived.reshape(ep_count * capacity, model_width), "req", axis=0, tiled=True
        ),
        w_gate,
        w_up,
        w_down,
    )
    summed = lax.psum_scatter(
        partial_value.astype(jnp.float32).astype(jnp.bfloat16),
        "req",
        scatter_dimension=0,
        tiled=True,
    ).astype(jnp.float32)
    summed = summed.reshape(ep_count, capacity, model_width)
    returned = lax.all_to_all(
        summed.astype(jnp.bfloat16), "ep", split_axis=0, concat_axis=0, tiled=True
    ).astype(summed.dtype)
    moe_out = lax.dot_general(
        combine,
        returned.reshape(ep_count * capacity, model_width),
        (((0,), (0,)), ((), ())),
        precision=lax.Precision.HIGHEST,
        preferred_element_type=jnp.float32,
    )
    return (attention_out, moe_out.astype(jnp.bfloat16))


def solution(mesh):
    placed = (
        P(("req", "ep"), None, None),
        P(("req", "ep"), None, None),
        P(("req", "ep"), None),
        P(),
        P(),
        P(("req", "ep"), None),
        P(("req", "ep"), None),
        P(("req", "ep"), None),
        P("ep", None, "req"),
        P("ep", None, "req"),
        P("ep", "req", None),
    )
    return jax.shard_map(
        body,
        mesh=mesh,
        in_specs=placed,
        out_specs=(P(("req", "ep"), None, None), P(("req", "ep"), None)),
        check_vma=False,
    )
```

profile of v0, /device:TPU:11, one launch (start us, length us, event | category | flops | bytes accessed | tf_op | source)
XLA Modules:
  0.0 215.4 jit_solution(4581101419035294104)
XLA Ops:
  7.2 0.8 eq.306
  8.5 0.7 multiply_add_fusion
  9.3 2.4 %convolution_convert_fusion = bf16[80,7168]{1,0:T(8,128)(2,1)} fusion(pred[80,8]{0,1:T(8,128)(4,1)S(1)} %fusion.31, bf16[8,7168]{1,0:T(8,128)(2,1)} %param.16), kind=kOutput, calls=%fused_computation.23 | convolution fusion | flops 9748480 | bytes 1262208 | tf_op jit(solution)/shard_map/dot_general | solution.py:118
  11.7 1.6 reshape.271
  13.3 48.1 %all_to_all.10 = bf16[16,5,7168]{2,1,0:T(8,128)(2,1)} all-to-all(bf16[16,5,7168]{2,1,0:T(8,128)(2,1)S(1)} %reshape.271), channel_id=1, replica_groups=mesh['req'=2,'ep'=16] {'ep'}, dimensions={0} | all-to-all | bytes 2293760 | tf_op jit(solution)/shard_map/all_to_all | solution.py:120
  61.4 2.6 %reshape.272 = bf16[80,7168]{1,0:T(8,128)(2,1)} reshape(bf16[16,5,7168]{2,1,0:T(8,128)(2,1)} %all_to_all.10) | data formatting | bytes 2293760 | tf_op jit(solution)/shard_map/reshape | solution.py:123
  69.4 29.5 %all-gather.2.cloned.1.call-done = bf16[160,7168]{1,0:T(8,128)(2,1)} async-done(((bf16[80,7168]{1,0:T(8,128)(2,1)}), bf16[160,7168]{1,0:T(8,128)(2,1)}) %all-gather.2.cloned.1.call-update) | async-done | bytes 2293776 | tf_op jit(solution)/shard_map/all_gather | solution.py:122
  98.9 8.5 %fusion.4 = f32[160,1024]{1,0:T(8,128)S(1)} fusion(bf16[160,7168]{1,0:T(8,128)(2,1)} %all-gather.2.cloned.1.call-done, bf16[1,7168,1024]{2,1,0:T(8,128)(2,1)} %param.19), kind=kOutput, calls=%fused_computation.20 | convolution fusion | flops 2348810240 | bytes 17629184 | tf_op jit(solution)/shard_map/dot_general | solution.py:35
  107.5 8.0 %fusion.22 = bf16[160,1024]{1,0:T(8,128)(2,1)S(1)} fusion(bf16[160,7168]{1,0:T(8,128)(2,1)S(1)} %copy-done.1, bf16[1,7168,1024]{2,1,0:T(8,128)(2,1)} %param.20, f32[160,1024]{1,0:T(8,128)S(1)} %fusion.4), kind=kOutput, calls=%fused_computation.40 | convolution fusion | flops 2349793280 | bytes 17956864 | tf_op jit(solution)/shard_map/dot_general | solution.py:36
  115.6 4.0 %fusion.6 = bf16[160,7168]{1,0:T(8,128)(2,1)} fusion(bf16[160,1024]{1,0:T(8,128)(2,1)S(1)} %fusion.22, bf16[1,1024,7168]{2,1,0:T(8,128)(2,1)S(1)} %bitcast.103), kind=kOutput, calls=%fused_computation.22 | convolution fusion | flops 2349957120 | bytes 17301504 | tf_op jit(solution)/shard_map/dot_general | solution.py:38
  128.5 25.3 %reduce-scatter.2.cloned.1.call-done = bf16[80,7168]{1,0:T(8,128)(2,1)} async-done(((bf16[160,7168]{1,0:T(8,128)(2,1)}), bf16[80,7168]{1,0:T(8,128)(2,1)}) %reduce-scatter.2.cloned.1.call-update) | async-done | bytes 1146896 | tf_op jit(solution)/shard_map/reduce_scatter | solution.py:129
  153.9 2.6 %convert_element_type.37 = bf16[16,5,7168]{2,1,0:T(8,128)(2,1)} reshape(bf16[80,7168]{1,0:T(8,128)(2,1)} %reduce-scatter.2.cloned.1.call-done) | data formatting | bytes 2293760 | tf_op jit(solution)/shard_map/convert_element_type | solution.py:137
  156.4 6.5 %all-to-all-start.1 = ((bf16[16,5,7168]{2,1,0:T(8,128)(2,1)}), bf16[16,5,7168]{2,1,0:T(8,128)(2,1)S(1)}, u32[]{:S(2)}, u32[]{:S(2)}) async-start(bf16[16,5,7168]{2,1,0:T(8,128)(2,1)} %convert_element_type.37), calls=%async_computation.2 | async-start | bytes 3670016 | tf_op jit(solution)/shard_map/all_to_all | solution.py:136
  163.6 1.4 copy.28
  165.0 1.0 broadcast_in_dim.21
  166.0 2.4 %copy.32 = pred[512,1040]{0,1:T(8,128)(4,1)} copy(pred[512,1040]{1,0:T(8,128)(4,1)} %bitcast.104) | data formatting | bytes 1064960 | tf_op jit(solution)/shard_map/jit(_where)/broadcast_in_dim | solution.py:96
  168.4 2.1 copy.29
  170.5 1.3 select_bitcast_fusion.1
  171.9 1.2 fusion.66
  173.8 1.4 copy.33
  175.2 3.2 %convolution_convert_fusion.2 = bf16[8,64,512]{2,1,0:T(8,128)(2,1)} fusion(bf16[8,64,1040]{2,1,0:T(8,128)(2,1)} %bitcast.105, bf16[8,576]{1,0:T(8,128)(2,1)} %copy-done.9, bf16[8,576]{1,0:T(8,128)(2,1)} %copy-done.8, bf16[512,576]{1,0:T(8,128)(2,1)} %copy-done.3, bf16[512,576]{1,0:T(8,128)(2,1)} %copy-done.2), kind=kOutput, calls=%fused_computation.38 | convolution fusion | flops 549781504 | bytes 2787328 | tf_op jit(solution)/shard_map/dot_general | solution.py:101
  178.4 26.3 %all-to-all-done.1 = bf16[16,5,7168]{2,1,0:T(8,128)(2,1)S(1)} async-done(((bf16[16,5,7168]{2,1,0:T(8,128)(2,1)}), bf16[16,5,7168]{2,1,0:T(8,128)(2,1)S(1)}, u32[]{:S(2)}, u32[]{:S(2)}) %all-to-all-start.1) | async-done | bytes 1146912 | tf_op jit(solution)/shard_map/all_to_all | solution.py:136
  204.8 1.4 reshape.273
  206.1 2.5 %convolution_convert_fusion.1 = bf16[8,7168]{1,0:T(8,128)(2,1)} fusion(f32[80,8]{0,1:T(8,128)S(1)} %copy-done.5, bf16[80,7168]{1,0:T(8,128)(2,1)} %reshape.273), kind=kOutput, calls=%fused_computation.24 | convolution fusion | flops 55107584 | bytes 1264128 | tf_op jit(solution)/shard_map/dot_general | solution.py:139
  (111 shorter events, 16.2 us)
Async XLA Ops:
  7.2 164.7 %copy-start = (bf16[8,64,576]{2,1,0:T(8,128)(2,1)S(1)}, bf16[8,64,576]{2,1,0:T(8,128)(2,1)}, u32[]{:S(2)}) copy-start(bf16[8,64,576]{2,1,0:T(8,128)(2,1)} %param.11) | copy-start | bytes 1769476
  7.2 91.7 %all-gather.2.cloned.1.call-start = ((), (), s32[]{:S(2)}) async-start(), calls=%async_computation.3 | async-start | bytes 3440640 | tf_op jit(solution)/shard_map/all_gather | solution.py:122
  61.4 2.8 %copy-start.7 = (bf16[8,576]{1,0:T(8,128)(2,1)S(1)}, bf16[8,576]{1,0:T(8,128)(2,1)}, u32[]{:S(2)}) copy-start(bf16[8,576]{1,0:T(8,128)(2,1)} %param.13) | copy-start | bytes 27652
  64.0 89.9 %reduce-scatter.2.cloned.1.call-start = ((), (), s32[]{:S(2)}) async-start(), calls=%async_computation.4 | async-start | bytes 3440640 | tf_op jit(solution)/shard_map/reduce_scatter | solution.py:129
  64.0 104.4 %collective-permute-start = (bf16[1,512,576]{1,2,0:T(8,128)(2,1)}, bf16[1,512,576]{1,2,0:T(8,128)(2,1)}, u32[]{:S(2)}, u32[]{:S(2)}) collective-permute-start(bf16[1,512,576]{1,2,0:T(8,128)(2,1)} %param.12), channel_id=1, source_target_pairs={{0,1},{1,0},{2,3},{3,2},{4,5},{5,4},{6,7},{7,6},{8,9},{9,8},{10,11... | collective-permute-start | bytes 1769480 | tf_op jit(solution)/shard_map/ppermute | solution.py:20
  64.2 104.2 %collective-permute-start.1 = (bf16[8,576]{1,0:T(8,128)(2,1)S(1)}, bf16[8,576]{1,0:T(8,128)(2,1)S(1)}, u32[]{:S(2)}, u32[]{:S(2)}) collective-permute-start(bf16[8,576]{1,0:T(8,128)(2,1)S(1)} %copy-done.7), channel_id=1, source_target_pairs={{0,1},{1,0},{2,3},{3,2},{4,5},{5,4},{6,7},{7,6},{8,9},{9,8},{10,11... | collective-permute-start | bytes 27656 | tf_op jit(solution)/shard_map/ppermute | solution.py:20
  98.9 8.6 %copy-start.1 = (bf16[160,7168]{1,0:T(8,128)(2,1)S(1)}, bf16[160,7168]{1,0:T(8,128)(2,1)}, u32[]{:S(2)}) copy-start(bf16[160,7168]{1,0:T(8,128)(2,1)} %all-gather.2.cloned.1.call-done) | copy-start | bytes 6881284
  98.9 16.6 %slice-start = ((s8[14680064]{0:T(1024)(128)(4,1)}), s8[4194304]{0:T(1024)(128)(4,1)S(1)}, s32[]{:S(2)}) async-start(s8[14680064]{0:T(1024)(128)(4,1)} %bitcast.102), calls=%async_computation.5 | async-start | bytes 8388608
  98.9 16.6 %slice-start.1 = ((s8[14680064]{0:T(1024)(128)(4,1)}), s8[4194304]{0:T(1024)(128)(4,1)S(1)}, s32[]{:S(2)}) async-start(s8[14680064]{0:T(1024)(128)(4,1)} %bitcast.102), calls=%async_computation.6 | async-start | bytes 8388608
  107.5 8.1 %slice-start.2 = ((s8[14680064]{0:T(1024)(128)(4,1)}), s8[4194304]{0:T(1024)(128)(4,1)S(1)}, s32[]{:S(2)}) async-start(s8[14680064]{0:T(1024)(128)(4,1)} %bitcast.102), calls=%async_computation.7 | async-start | bytes 8388608
  107.5 8.1 %slice-start.3 = ((s8[14680064]{0:T(1024)(128)(4,1)}), s8[2097152]{0:T(1024)(128)(4,1)S(1)}, s32[]{:S(2)}) async-start(s8[14680064]{0:T(1024)(128)(4,1)} %bitcast.102), calls=%async_computation.8 | async-start | bytes 4194304
  121.0 5.8 %copy-start.10 = (s32[16]{0:T(128)S(1)}, s32[16]{0:T(128)}, u32[]{:S(2)}) copy-start(s32[16]{0:T(128)} %param.15) | copy-start | bytes 196
  121.0 7.3 %copy-start.6 = (f32[8,8]{1,0:T(8,128)S(1)}, f32[8,8]{1,0:T(8,128)}, u32[]{:S(2)}) copy-start(f32[8,8]{1,0:T(8,128)} %param.18) | copy-start | bytes 772
  156.4 48.3 %all-to-all-start.1 = ((bf16[16,5,7168]{2,1,0:T(8,128)(2,1)}), bf16[16,5,7168]{2,1,0:T(8,128)(2,1)S(1)}, u32[]{:S(2)}, u32[]{:S(2)}) async-start(bf16[16,5,7168]{2,1,0:T(8,128)(2,1)} %convert_element_type.37), calls=%async_computation.2 | async-start | bytes 3670016 | tf_op jit(solution)/shard_map/all_to_all | solution.py:136
  168.4 4.6 %copy-start.8 = (bf16[8,576]{1,0:T(8,128)(2,1)}, bf16[8,576]{1,0:T(8,128)(2,1)S(1)}, u32[]{:S(2)}) copy-start(bf16[8,576]{1,0:T(8,128)(2,1)S(1)} %get-tuple-element.4) | copy-start | bytes 27652
  168.4 4.6 %copy-start.9 = (bf16[8,576]{1,0:T(8,128)(2,1)}, bf16[8,576]{1,0:T(8,128)(2,1)S(1)}, u32[]{:S(2)}) copy-start(bf16[8,576]{1,0:T(8,128)(2,1)S(1)} %get-tuple-element.5) | copy-start | bytes 27652
  170.5 1.3 copy-start.4
  171.8 1.2 copy-start.2
  171.8 1.2 copy-start.3
  178.4 27.7 %copy-start.5 = (f32[80,8]{0,1:T(8,128)S(1)}, f32[80,8]{0,1:T(8,128)}, u32[]{:S(2)}) copy-start(f32[80,8]{0,1:T(8,128)} %select_reduce_fusion) | copy-start | bytes 7684
Sparse Core Ops, SparseCore 0:
  64.1 34.7 all-gather.1
  119.8 34.0 reduce-scatter.1
where the time goes:
time: 216 us; the launch traced here: 215 us
  waiting for transfers between devices  81.2 us (38%)
  blocking collectives  48.1 us (22%)
  matrix products  29.8 us (14%)
  local copies, waits for them, and re-layouts  29.5 us (14%)
  between operations  14.4 us (7%)
  starting transfers between devices  7.17 us (3%)
  other arithmetic  5.09 us (2%)
    all_to_all x1, blocking collectives, body(): lax.all_to_all(outgoing, 'ep', split_axis=0, concat_axis=0, tiled=True)  48.1 us
    all_gather x1, waiting for transfers between devices, body(): lax.all_gather(arrived.reshape(ep_count * capacity, model_width), 'req',...  29.5 us
    all_to_all x1, waiting for transfers between devices, body(): lax.all_to_all(summed.astype(jnp.bfloat16), 'ep', split_axis=0, concat_ax...  26.3 us
    reduce_scatter x1, waiting for transfers between devices, body(): lax.psum_scatter(partial_value.astype(jnp.float32).astype(jnp.bfloat16),...  25.3 us
    gather x16, local copies, waits for them, and re-layouts, ancestor_table(): current = parent_row[current]  10.5 us
    dot_general x1, matrix products, expert_mlp(): gate_val = jnp.dot(row_block, w_gate[0], preferred_element_type=jnp.float32)  8.54 us
    dot_general x1, matrix products, expert_mlp(): up_val = jnp.dot(row_block, w_up[0], preferred_element_type=jnp.float32)  8.03 us
    all_to_all x1, starting transfers between devices, body(): lax.all_to_all(summed.astype(jnp.bfloat16), 'ep', split_axis=0, concat_ax...  6.51 us
  transfers between devices with their start and end apart: 5, of which 3 were waited for; matrix products, arithmetic and copies ran while one was open for 24% of the time, Pallas kernels for 0%

commit v1 on v0

v1 whole, which is shorter than its diff:
```python
import functools

import jax
import jax.numpy as jnp
from jax import lax
from jax.experimental import pallas as pl
from jax.experimental.pallas import tpu as pltpu
from jax.sharding import PartitionSpec as P

VDIM = 512
AXES = ("req", "ep")
NEG = -1e30

score_scale = 192.0 ** (-0.5)
route_scale = 2.5


def swap(block, count, partner):
    return lax.ppermute(block, AXES, [(i, partner(i)) for i in range(count)])


def pack_kernel(ep_count, tokens_ref, ids_ref, scores_ref, mine_ref, theirs_ref):
    core = lax.axis_index("ep") % 2
    half = tokens_ref.shape[1] // 2
    extra = mine_ref.shape[1] - half
    scores = scores_ref[...]
    weight = route_scale * scores / jnp.sum(scores, axis=1, keepdims=True)
    ids = ids_ref[...]
    lane = lax.broadcasted_iota(jnp.int32, (ids.shape[0], extra), 1)
    expert = jnp.where(lane >= ep_count, lane - ep_count, lane)
    dense = jnp.zeros(lane.shape, jnp.float32)
    for k in range(ids.shape[1]):
        dense = dense + jnp.where(ids[:, k : k + 1] == expert, weight[:, k : k + 1], 0.0)
    high = dense.astype(jnp.bfloat16)
    low = (dense - high.astype(jnp.float32)).astype(jnp.bfloat16)
    packed = jnp.where(
        lane < ep_count, high.astype(jnp.float32), jnp.where(lane < 2 * ep_count, low.astype(jnp.float32), 0.0)
    ).astype(jnp.bfloat16)
    first = tokens_ref[:, :half]
    second = tokens_ref[:, half:]
    even = core == 0
    mine_ref[:, :half] = jnp.where(even, first, second)
    theirs_ref[:, :half] = jnp.where(even, second, first)
    mine_ref[:, half:] = packed
    theirs_ref[:, half:] = packed


def pack(tokens, route_ids, route_scores, ep_count, extra):
    rows, width = tokens.shape
    out = jax.ShapeDtypeStruct((rows, width // 2 + extra), jnp.bfloat16)
    return pl.pallas_call(
        functools.partial(pack_kernel, ep_count),
        out_shape=(out, out),
        name="pack",
    )(tokens, route_ids, route_scores)


def attention_kernel(
    where_ref, parents_ref, length_ref, q_ref, own_ref, other_ref, fresh_ref, other_fresh_ref, out_ref, line_ref
):
    half_index, request = where_ref[0], where_ref[1]
    nodes = line_ref.shape[0]
    tok_dev = nodes // 2
    rows = q_ref.shape[0]
    heads = rows // (tok_dev // pl.num_programs(0))
    length = length_ref[request]
    line_ref[0] = 1
    for node in range(1, nodes):
        line_ref[node] = (1 << node) | line_ref[parents_ref[request, node]]
    span = own_ref.shape[1]
    queries = q_ref[...]
    column = lax.broadcasted_iota(jnp.int32, (1, span), 1)
    dims = (((1,), (0,)), ((), ()))
    flipped = (((1,), (1,)), ((), ()))

    def masked(keys_ref, start):
        scores = lax.dot_general(queries, keys_ref[...], dims, preferred_element_type=jnp.float32) * score_scale
        return jnp.where(column + start < length, scores, NEG)

    scores_own = masked(own_ref, half_index * span)
    scores_other = masked(other_ref, (1 - half_index) * span)

    def tree(keys_ref, first_key):
        scores = lax.dot_general(queries, keys_ref[...], flipped, preferred_element_type=jnp.float32) * score_scale
        key = first_key + lax.broadcasted_iota(jnp.int32, (heads, tok_dev), 1)
        pieces = []
        for t in range(rows // heads):
            node = half_index * tok_dev + pl.program_id(0) * (rows // heads) + t
            ancestors = line_ref[node]
            pieces.append(
                jnp.where((jnp.full(key.shape, ancestors, jnp.int32) >> key) & 1 == 1, scores[t * heads : (t + 1) * heads], NEG)
            )
        return jnp.concatenate(pieces, axis=0)

    scores_fresh = tree(fresh_ref, half_index * tok_dev)
    scores_fresh_other = tree(other_fresh_ref, (1 - half_index) * tok_dev)
    parts = (scores_own, scores_other, scores_fresh, scores_fresh_other)
    top = functools.reduce(jnp.maximum, [jnp.max(part, axis=1, keepdims=True) for part in parts])
    weights = [jnp.exp(part - top) for part in parts]
    total = functools.reduce(jnp.add, [jnp.sum(part, axis=1, keepdims=True) for part in weights])
    vdim = out_ref.shape[1]
    out = lax.dot_general(
        weights[0].astype(jnp.bfloat16), own_ref[:vdim, :], flipped, preferred_element_type=jnp.float32
    )
    out += lax.dot_general(
        weights[1].astype(jnp.bfloat16), other_ref[:vdim, :], flipped, preferred_element_type=jnp.float32
    )
    out += lax.dot_general(
        weights[2].astype(jnp.bfloat16), fresh_ref[:, :vdim], dims, preferred_element_type=jnp.float32
    )
    out += lax.dot_general(
        weights[3].astype(jnp.bfloat16), other_fresh_ref[:, :vdim], dims, preferred_element_type=jnp.float32
    )
    out_ref[...] = (out / total).astype(out_ref.dtype)


def attention(queries, own, other, fresh, other_fresh, parents, cache_len, half_index, request):
    tok_dev, heads, width = queries.shape
    rows = tok_dev * heads
    steps = 2
    whole = lambda array: pl.BlockSpec(array.shape, lambda i, *_: (0,) * array.ndim)
    out = pl.pallas_call(
        attention_kernel,
        out_shape=jax.ShapeDtypeStruct((rows, VDIM), jnp.bfloat16),
        grid_spec=pltpu.PrefetchScalarGridSpec(
            num_scalar_prefetch=3,
            grid=(steps,),
            in_specs=[
                pl.BlockSpec((rows // steps, width), lambda i, *_: (i, 0)),
                whole(own),
                whole(other),
                whole(fresh),
                whole(other_fresh),
            ],
            out_specs=pl.BlockSpec((rows // steps, VDIM), lambda i, *_: (i, 0)),
            scratch_shapes=[pltpu.SMEM((parents.shape[1],), jnp.int32)],
        ),
        cost_estimate=pl.CostEstimate(
            flops=2 * rows * 1040 * (width + VDIM), bytes_accessed=3 * 1024 * 1024, transcendentals=rows * 1040
        ),
        name="attention",
    )(
        jnp.stack([half_index, request]).astype(jnp.int32),
        parents,
        cache_len,
        queries.reshape(rows, width),
        own,
        other,
        fresh,
        other_fresh,
    )
    return out.reshape(tok_dev, heads, VDIM)


def gate_up_kernel(
    steps, ep_count, core_ref, mine_lo, mine_hi, other_lo, other_hi, side_lo, side_hi, gate_ref, up_ref, out_ref, gate_acc, up_acc
):
    step = pl.program_id(0)
    quarter = mine_lo.shape[0] // 2
    rows = mine_lo.shape[0]

    @pl.when(step == 0)
    def _():
        gate_acc[...] = jnp.zeros_like(gate_acc)
        up_acc[...] = jnp.zeros_like(up_acc)

    def add(start, block):
        at = pl.ds(start, block.shape[0])
        gate_acc[at, :] += jnp.dot(block, gate_ref[...], preferred_element_type=jnp.float32)
        up_acc[at, :] += jnp.dot(block, up_ref[...], preferred_element_type=jnp.float32)

    @pl.when(step < steps)
    def _():
        add(0, jnp.concatenate([mine_lo[...], mine_hi[...]], axis=0))

    @pl.when(step >= steps)
    def _():
        add(
            0,
            jnp.concatenate(
                [other_lo[:quarter, :], other_hi[:quarter, :], other_lo[quarter:, :], other_hi[quarter:, :]], axis=0
            ),
        )

    @pl.when(step == 2 * steps - 1)
    def _():
        expert = core_ref[1]
        for start, side in ((0, side_lo), (rows, side_hi)):
            at = pl.ds(start, rows)
            values = side[...].astype(jnp.float32)
            lane = lax.broadcasted_iota(jnp.int32, values.shape, 1)
            hit = (lane == expert) | (lane == expert + ep_count)
            weight = jnp.sum(jnp.where(hit, values, 0.0), axis=1, keepdims=True)
            gate = gate_acc[at, :]
            out_ref[at, :] = (gate / (1.0 + jnp.exp(-gate)) * up_acc[at, :] * weight).astype(out_ref.dtype)


def gate_up(place, mine_lo, mine_hi, other_lo, other_hi, w_gate, w_up, ep_count, half):
    rows, width = mine_lo.shape
    hidden = w_gate.shape[1]
    tile = half // 2
    steps = half // tile
    extra = width - half
    own = pl.BlockSpec((rows, tile), lambda k, p: (0, jnp.minimum(k, steps - 1)))
    other = pl.BlockSpec((rows, tile), lambda k, p: (0, jnp.maximum(k - steps, 0)))
    side = pl.BlockSpec((rows, extra), lambda k, p: (0, half // extra))
    weight = pl.BlockSpec((tile, hidden), lambda k, p: (jnp.where(k < steps, p[0] * steps + k, (1 - p[0]) * steps + k - steps), 0))
    return pl.pallas_call(
        functools.partial(gate_up_kernel, steps, ep_count),
        out_shape=jax.ShapeDtypeStruct((2 * rows, hidden), jnp.bfloat16),
        grid_spec=pltpu.PrefetchScalarGridSpec(
            num_scalar_prefetch=1,
            grid=(2 * steps,),
            in_specs=[own, own, other, other, side, side, weight, weight],
            out_specs=pl.BlockSpec((2 * rows, hidden), lambda k, p: (0, 0)),
            scratch_shapes=[pltpu.VMEM((2 * rows, hidden), jnp.float32)] * 2,
        ),
        compiler_params=pltpu.CompilerParams(vmem_limit_bytes=48 * 1024 * 1024),
        cost_estimate=pl.CostEstimate(
            flops=8 * rows * half * 2 * hidden, bytes_accessed=8 * half * hidden, transcendentals=2 * rows * hidden
        ),
        name="gate_up",
    )(place, mine_lo, mine_hi, other_lo, other_hi, mine_lo, mine_hi, w_gate, w_up)


def down_kernel(theirs, place_ref, hidden_ref, weight_ref, low_ref, high_ref):
    out = jnp.dot(hidden_ref[...], weight_ref[...], preferred_element_type=jnp.float32).astype(low_ref.dtype)
    rows = low_ref.shape[0]
    quarter = rows // 2
    if theirs:
        low_ref[:quarter, :] = out[:quarter]
        low_ref[quarter:, :] = out[rows : rows + quarter]
        high_ref[:quarter, :] = out[quarter:rows]
        high_ref[quarter:, :] = out[rows + quarter :]
    else:
        low_ref[...] = out[:rows]
        high_ref[...] = out[rows:]


def down(place, hidden, w_down, half, theirs):
    rows, depth = hidden.shape
    tile = half // 2
    steps = half // tile
    side = (lambda p: 1 - p[0]) if theirs else (lambda p: p[0])
    out = jax.ShapeDtypeStruct((rows // 2, half), jnp.bfloat16)
    out_spec = pl.BlockSpec((rows // 2, tile), lambda n, p: (0, n))
    return pl.pallas_call(
        functools.partial(down_kernel, theirs),
        out_shape=(out, out),
        grid_spec=pltpu.PrefetchScalarGridSpec(
            num_scalar_prefetch=1,
            grid=(steps,),
            in_specs=[
                pl.BlockSpec((rows, depth), lambda n, p: (0, 0)),
                pl.BlockSpec((depth, tile), lambda n, p: (0, side(p) * steps + n)),
            ],
            out_specs=(out_spec, out_spec),
        ),
        compiler_params=pltpu.CompilerParams(vmem_limit_bytes=32 * 1024 * 1024),
        cost_estimate=pl.CostEstimate(
            flops=2 * rows * depth * half, bytes_accessed=2 * depth * half, transcendentals=0
        ),
        name="down_theirs" if theirs else "down_mine",
    )(place, hidden, w_down)


def body(
    queries,
    latent_cache,
    new_latents,
    parents,
    cache_len,
    tokens,
    route_ids,
    route_scores,
    w_gate,
    w_up,
    w_down,
):
    ep_count = lax.axis_size("ep")
    count = lax.axis_size("req") * ep_count
    bits = count.bit_length() - 1
    assert count == 1 << bits and bits >= 4
    expert = lax.axis_index("ep")
    position = lax.axis_index("req") * ep_count + expert
    core = position % 2
    even = core == 0
    first, last = 2, 1 << (bits - 1)
    group = 1 << (bits - 3)

    def trade_pair(block):
        return swap(block, count, lambda i: i ^ 1)

    def trade_near(block):
        return swap(block, count, lambda i: i ^ (first if i % 2 == 0 else last))

    def trade_far(block):
        return swap(block, count, lambda i: i ^ (last if i % 2 == 0 else first))

    def trade_group(block, offset):
        return swap(block, count, lambda i: i ^ (offset * 4))

    half = tokens.shape[1] // 2
    extra = -(-2 * ep_count // 128) * 128
    place = jnp.stack([core, expert]).astype(jnp.int32)

    mine, theirs = pack(tokens, route_ids, route_scores, ep_count, extra)
    got = trade_pair(theirs)
    pair = jnp.concatenate([jnp.where(even, mine, got), jnp.where(even, got, mine)], axis=0)
    line = jnp.concatenate([pair] + [trade_group(pair, j) for j in range(1, group)], axis=0)
    low = jnp.concatenate([line, trade_near(line)], axis=0)
    high = trade_far(low)
    other_low = trade_pair(low)
    other_high = trade_pair(high)

    cache = jnp.swapaxes(latent_cache[0], 0, 1)
    other_cache, other_fresh = trade_pair(cache), trade_pair(new_latents)
    attention_out = attention(
        queries, cache, other_cache, new_latents, other_fresh, parents, cache_len, core, position // 2
    )

    hidden = gate_up(place, low, high, other_low, other_high, w_gate[0], w_up[0], ep_count, half)
    send_low, send_high = down(place, hidden, w_down[0], half, True)
    keep_low, keep_high = down(place, hidden, w_down[0], half, False)

    def add(*blocks):
        return functools.reduce(jnp.add, [block.astype(jnp.float32) for block in blocks])

    def rounded(*blocks):
        return add(*blocks).astype(jnp.bfloat16)

    back_high = trade_pair(send_high)
    back_low = trade_pair(send_low)
    far = trade_far(rounded(keep_high, back_high))
    quarter = keep_low.shape[0] // 2
    near = trade_near(rounded(keep_low[quarter:], back_low[quarter:], far[quarter:]))
    rows = quarter // group
    sums = rounded(keep_low[:quarter], back_low[:quarter], far[:quarter], near)
    parts = [sums[:rows]] + [trade_group(sums[j * rows : (j + 1) * rows], j) for j in range(1, group)]
    total = rounded(*parts)
    tok_dev = tokens.shape[0]
    keep = jnp.where(even, total[:tok_dev], total[tok_dev:])
    give = jnp.where(even, total[tok_dev:], total[:tok_dev])
    given = trade_pair(give)
    moe_out = jnp.concatenate([jnp.where(even, keep, given), jnp.where(even, given, keep)], axis=1)
    return (attention_out, moe_out)


def solution(mesh):
    placed = (
        P(("req", "ep"), None, None),
        P(("req", "ep"), None, None),
        P(("req", "ep"), None),
        P(),
        P(),
        P(("req", "ep"), None),
        P(("req", "ep"), None),
        P(("req", "ep"), None),
        P("ep", None, "req"),
        P("ep", None, "req"),
        P("ep", "req", None),
    )
    return jax.shard_map(
        body,
        mesh=mesh,
        in_specs=placed,
        out_specs=(P(("req", "ep"), None, None), P(("req", "ep"), None)),
        check_vma=False,
    )
```

time: 216 us -> 115 us (0.53)
  blocking collectives: 48.1 us -> 0 us
  matrix products: 29.8 us -> 0 us
  Pallas kernels: 0 us -> 28.5 us
  waiting for transfers between devices: 81.2 us -> 53.6 us
  local copies, waits for them, and re-layouts: 29.5 us -> 6.15 us
  starting transfers between devices: 7.17 us -> 21.7 us
  between operations: 14.4 us -> 0.78 us
    ppermute x2 -> x18, waiting for transfers between devices: 0.01 us -> 53.6 us  [swap(): return lax.ppermute(block, AXES, [(i, partner(i)) for i in range(count)])]
    all_to_all x1 -> x0, blocking collectives: 48.1 us -> none  [body(): lax.all_to_all(outgoing, 'ep', split_axis=0, concat_axis=0, tiled=True)]
    dot_general x7 -> x0, matrix products: 29.8 us -> none  [the longest x1 8.54 us: expert_mlp(): gate_val = jnp.dot(row_block, w_gate[0], preferred_element_type=jnp.float32)]
    all_gather x1 -> x0, waiting for transfers between devices: 29.5 us -> none  [body(): lax.all_gather(arrived.reshape(ep_count * capacity, model_width), 'req',...]
    pallas_call x0 -> x5, Pallas kernels: none -> 28.5 us  [the longest x1 14.2 us: gate_up(): pl.pallas_call(functools.partial(gate_up_kernel, steps, ep_count), out_sh...]
    all_to_all x1 -> x0, waiting for transfers between devices: 26.3 us -> none  [body(): lax.all_to_all(summed.astype(jnp.bfloat16), 'ep', split_axis=0, concat_ax...]
    reduce_scatter x1 -> x0, waiting for transfers between devices: 25.3 us -> none  [body(): lax.psum_scatter(partial_value.astype(jnp.float32).astype(jnp.bfloat16),...]
    ppermute x2 -> x18, starting transfers between devices: 0.58 us -> 21.7 us  [swap(): return lax.ppermute(block, AXES, [(i, partner(i)) for i in range(count)])]
  transfers between devices with their start and end apart: 5 -> 18, of which waited for: 3 -> 11; matrix products, arithmetic and copies ran while one was open for 24% -> 1% of each run, Pallas kernels for 0% -> 8%
where the time goes in v1:
time: 115 us; the launch traced here: 114 us
  waiting for transfers between devices  53.6 us (47%)
  Pallas kernels  28.5 us (25%)
  starting transfers between devices  21.7 us (19%)
  local copies, waits for them, and re-layouts  6.15 us (5%)
  other arithmetic  2.96 us (3%)
    ppermute x18, waiting for transfers between devices, swap(): return lax.ppermute(block, AXES, [(i, partner(i)) for i in range(count)])  53.6 us
    ppermute x18, starting transfers between devices, swap(): return lax.ppermute(block, AXES, [(i, partner(i)) for i in range(count)])  21.7 us
    pallas_call x1, Pallas kernels, gate_up(): pl.pallas_call(functools.partial(gate_up_kernel, steps, ep_count), out_sh...  14.2 us
    pallas_call x2, Pallas kernels, down(): pl.pallas_call(functools.partial(down_kernel, theirs), out_shape=(out, ou...  6.85 us
    unnamed x14, local copies, waits for them, and re-layouts  6.06 us
    pallas_call x1, Pallas kernels, attention(): pl.pallas_call(attention_kernel, out_shape=jax.ShapeDtypeStruct((rows, VD...  5.69 us
  transfers between devices with their start and end apart: 18, of which 11 were waited for; matrix products, arithmetic and copies ran while one was open for 1% of the time, Pallas kernels for 8%

profile of v1, /device:TPU:11, one launch (start us, length us, event | category | flops | bytes accessed | tf_op | source)
XLA Modules:
  0.0 113.8 jit_solution(2056629732505787899)
XLA Ops:
  0.6 1.7 %pack.1 = (bf16[8,3712]{1,0:T(8,128)(2,1)}, bf16[8,3712]{1,0:T(8,128)(2,1)}) custom-call(bf16[8,7168]{1,0:T(8,128)(2,1)} %tokens_ref.1, s32[8,8]{1,0:T(8,128)} %ids_ref.1, f32[8,8]{1,0:T(8,128)} %scores_ref.1), custom_call_target="tpu_custom_call" | custom-call | tf_op jit(solution)/shard_map/pack/pallas_call | solution.py:51
  5.3 2.3 %collective-permute-start.4 = (bf16[16,3712]{1,0:T(8,128)(2,1)S(1)}, bf16[16,3712]{1,0:T(8,128)(2,1)S(1)}, u32[]{:S(2)}, u32[]{:S(2)}) collective-permute-start(bf16[16,3712]{1,0:T(8,128)(2,1)S(1)} %pad_maximum_fusion), channel_id=1, source_target_pairs={{0,8},{1,9},{2,10},{3,11},{4,12},{5,13},{6,14},{7,15},{8,0},{9,1},... | collective-permute-start | bytes 356360 | tf_op jit(solution)/shard_map/ppermute | solution.py:19
  7.8 1.8 %collective-permute-done.3 = bf16[16,3712]{1,0:T(8,128)(2,1)S(1)} collective-permute-done((bf16[16,3712]{1,0:T(8,128)(2,1)S(1)}, bf16[16,3712]{1,0:T(8,128)(2,1)S(1)}, u32[]{:S(2)}, u32[]{:S(2)}) %collective-permute-start.3) | collective-permute-done | bytes 118816 | tf_op jit(solution)/shard_map/ppermute | solution.py:19
  9.6 3.5 %collective-permute-done.4 = bf16[16,3712]{1,0:T(8,128)(2,1)S(1)} collective-permute-done((bf16[16,3712]{1,0:T(8,128)(2,1)S(1)}, bf16[16,3712]{1,0:T(8,128)(2,1)S(1)}, u32[]{:S(2)}, u32[]{:S(2)}) %collective-permute-start.4) | collective-permute-done | bytes 118816 | tf_op jit(solution)/shard_map/ppermute | solution.py:19
  13.2 5.0 %collective-permute-done.5 = bf16[16,3712]{1,0:T(8,128)(2,1)S(1)} collective-permute-done((bf16[16,3712]{1,0:T(8,128)(2,1)S(1)}, bf16[16,3712]{1,0:T(8,128)(2,1)S(1)}, u32[]{:S(2)}, u32[]{:S(2)}) %collective-permute-start.5) | collective-permute-done | bytes 118816 | tf_op jit(solution)/shard_map/ppermute | solution.py:19
  18.2 1.3 %collective-permute-start.6 = (bf16[64,3712]{1,0:T(8,128)(2,1)S(1)}, bf16[64,3712]{1,0:T(8,128)(2,1)S(1)}, u32[]{:S(2)}, u32[]{:S(2)}) collective-permute-start(bf16[64,3712]{1,0:T(8,128)(2,1)S(1)} %get-tuple-element.23), channel_id=1, source_target_pairs={{0,2},{1,17},{2,0},{3,19},{4,6},{5,21},{6,4},{7,23},{8,10},{9,25},... | collective-permute-start | bytes 1425416 | tf_op jit(solution)/shard_map/ppermute | solution.py:19
  19.5 6.6 %collective-permute-done.6 = bf16[64,3712]{1,0:T(8,128)(2,1)S(1)} collective-permute-done((bf16[64,3712]{1,0:T(8,128)(2,1)S(1)}, bf16[64,3712]{1,0:T(8,128)(2,1)S(1)}, u32[]{:S(2)}, u32[]{:S(2)}) %collective-permute-start.6) | collective-permute-done | bytes 475168 | tf_op jit(solution)/shard_map/ppermute | solution.py:19
  26.5 3.6 %collective-permute-start.8 = (bf16[128,3712]{1,0:T(8,128)(2,1)S(1)}, bf16[128,3712]{1,0:T(8,128)(2,1)S(1)}, u32[]{:S(2)}, u32[]{:S(2)}) collective-permute-start(bf16[128,3712]{1,0:T(8,128)(2,1)S(1)} %constant_dynamic-update-slice_fusion.5.mine_lo.side_lo), channel_id=1, source_target_pairs={{0,1},{1,0},{2,3},{3,2},{4,5},{5,4},{6,7},{7,6},{8,9},{9,8},{10,11... | collective-permute-start | bytes 2850824 | tf_op jit(solution)/shard_map/ppermute | solution.py:19
  30.0 9.1 %collective-permute-done.7.mine_hi.side_hi = bf16[128,3712]{1,0:T(8,128)(2,1)S(1)} collective-permute-done((bf16[128,3712]{1,0:T(8,128)(2,1)S(1)}, bf16[128,3712]{1,0:T(8,128)(2,1)S(1)}, u32[]{:S(2)}, u32[]{:S(2)}) %collective-permute-start.7) | collective-permute-done | bytes 950304 | tf_op jit(solution)/shard_map/ppermute | solution.py:19
  39.1 3.2 %collective-permute-start.9 = (bf16[128,3712]{1,0:T(8,128)(2,1)S(1)}, bf16[128,3712]{1,0:T(8,128)(2,1)S(1)}, u32[]{:S(2)}, u32[]{:S(2)}) collective-permute-start(bf16[128,3712]{1,0:T(8,128)(2,1)S(1)} %collective-permute-done.7.mine_hi.side_hi), channel_id=1, source_target_pairs={{0,1},{1,0},{2,3},{3,2},{4,5},{5,4},{6,7},{7,6},{8,9},{9,8},{10,11... | collective-permute-start | bytes 2850824 | tf_op jit(solution)/shard_map/ppermute | solution.py:19
  42.3 2.1 %collective-permute-done.9.other_hi = bf16[128,3712]{1,0:T(8,128)(2,1)S(1)} collective-permute-done((bf16[128,3712]{1,0:T(8,128)(2,1)S(1)}, bf16[128,3712]{1,0:T(8,128)(2,1)S(1)}, u32[]{:S(2)}, u32[]{:S(2)}) %collective-permute-start.9) | collective-permute-done | bytes 950304 | tf_op jit(solution)/shard_map/ppermute | solution.py:19
  44.4 14.2 %gate_up.1.hidden_ref = bf16[256,1024]{1,0:T(8,128)(2,1)S(1)} custom-call(s32[2]{0:T(128)S(1)} %pad_add_fusion.1.core_ref.place_ref, bf16[128,3712]{1,0:T(8,128)(2,1)S(1)} %constant_dynamic-update-slice_fusion.5.mine_lo.side_lo, bf16[128,3712]{1,0:T(8,128)(2,1)S(1)} %collective-permute-done.7.mine_hi.side_hi, ...), custom_call_target="tpu_custom_call" | custom-call | flops 7516192768 | bytes 29360128 | tf_op jit(solution)/shard_map/gate_up/pallas_call | solution.py:208
  58.6 5.2 %copy-done = bf16[1,1024,7168]{2,1,0:T(8,128)(2,1)S(1)} copy-done((bf16[1,1024,7168]{2,1,0:T(8,128)(2,1)S(1)}, bf16[1,1024,7168]{2,1,0:T(8,128)(2,1)}, u32[]{:S(2)}) %copy-start) | copy-done | bytes 14680088
  63.8 3.4 %down_theirs.1 = (bf16[128,3584]{1,0:T(8,128)(2,1)S(1)}, bf16[128,3584]{1,0:T(8,128)(2,1)S(1)}) custom-call(s32[2]{0:T(128)S(1)} %pad_add_fusion.1.core_ref.place_ref, bf16[256,1024]{1,0:T(8,128)(2,1)S(1)} %gate_up.1.hidden_ref, bf16[1024,7168]{1,0:T(8,128)(2,1)S(1)} %bitcast.11), custom_call_target="tpu_custom_call" | custom-call | flops 1879048192 | bytes 7340032 | tf_op jit(solution)/shard_map/down_theirs/pallas_call | solution.py:247
  67.9 3.4 %down_mine.1 = (bf16[128,3584]{1,0:T(8,128)(2,1)S(1)}, bf16[128,3584]{1,0:T(8,128)(2,1)S(1)}) custom-call(s32[2]{0:T(128)S(1)} %pad_add_fusion.1.core_ref.place_ref, bf16[256,1024]{1,0:T(8,128)(2,1)S(1)} %gate_up.1.hidden_ref, bf16[1024,7168]{1,0:T(8,128)(2,1)S(1)} %bitcast.12), custom_call_target="tpu_custom_call" | custom-call | flops 1879048192 | bytes 7340032 | tf_op jit(solution)/shard_map/down_mine/pallas_call | solution.py:247
  71.8 12.3 %collective-permute-done.12 = bf16[128,3584]{1,0:T(8,128)(2,1)S(1)} collective-permute-done((bf16[128,3584]{1,0:T(8,128)(2,1)S(1)}, bf16[128,3584]{1,0:T(8,128)(2,1)S(1)}, u32[]{:S(2)}, u32[]{:S(2)}) %collective-permute-start.12) | collective-permute-done | bytes 917536 | tf_op jit(solution)/shard_map/ppermute | solution.py:19
  84.3 1.3 %collective-permute-start.13 = (bf16[64,3584]{1,0:T(8,128)(2,1)S(1)}, bf16[64,3584]{1,0:T(8,128)(2,1)S(1)}, u32[]{:S(2)}, u32[]{:S(2)}) collective-permute-start(bf16[64,3584]{1,0:T(8,128)(2,1)S(1)} %add_convert_fusion.2), channel_id=1, source_target_pairs={{0,2},{1,17},{2,0},{3,19},{4,6},{5,21},{6,4},{7,23},{8,10},{9,25},... | collective-permute-start | bytes 1376264 | tf_op jit(solution)/shard_map/ppermute | solution.py:19
  85.6 6.4 %collective-permute-done.13 = bf16[64,3584]{1,0:T(8,128)(2,1)S(1)} collective-permute-done((bf16[64,3584]{1,0:T(8,128)(2,1)S(1)}, bf16[64,3584]{1,0:T(8,128)(2,1)S(1)}, u32[]{:S(2)}, u32[]{:S(2)}) %collective-permute-start.13) | collective-permute-done | bytes 458784 | tf_op jit(solution)/shard_map/ppermute | solution.py:19
  92.3 2.5 %collective-permute-start.15 = (bf16[16,3584]{1,0:T(8,128)(2,1)S(1)}, bf16[16,3584]{1,0:T(8,128)(2,1)S(1)}, u32[]{:S(2)}, u32[]{:S(2)}) collective-permute-start(bf16[16,3584]{1,0:T(8,128)(2,1)S(1)} %get-tuple-element.20), channel_id=1, source_target_pairs={{0,8},{1,9},{2,10},{3,11},{4,12},{5,13},{6,14},{7,15},{8,0},{9,1},... | collective-permute-start | bytes 344072 | tf_op jit(solution)/shard_map/ppermute | solution.py:19
  95.0 2.9 %collective-permute-start = (bf16[576,512]{1,0:T(8,128)(2,1)S(1)}, bf16[576,512]{1,0:T(8,128)(2,1)S(1)}, u32[]{:S(2)}, u32[]{:S(2)}) collective-permute-start(bf16[576,512]{1,0:T(8,128)(2,1)S(1)} %bitcast.17), channel_id=1, source_target_pairs={{0,1},{1,0},{2,3},{3,2},{4,5},{5,4},{6,7},{7,6},{8,9},{9,8},{10,11... | collective-permute-start | bytes 1769480 | tf_op jit(solution)/shard_map/ppermute | solution.py:19
  98.6 3.1 %collective-permute-done.15 = bf16[16,3584]{1,0:T(8,128)(2,1)S(1)} collective-permute-done((bf16[16,3584]{1,0:T(8,128)(2,1)S(1)}, bf16[16,3584]{1,0:T(8,128)(2,1)S(1)}, u32[]{:S(2)}, u32[]{:S(2)}) %collective-permute-start.15) | collective-permute-done | bytes 114720 | tf_op jit(solution)/shard_map/ppermute | solution.py:19
  101.7 2.7 %collective-permute-done.16 = bf16[16,3584]{1,0:T(8,128)(2,1)S(1)} collective-permute-done((bf16[16,3584]{1,0:T(8,128)(2,1)S(1)}, bf16[16,3584]{1,0:T(8,128)(2,1)S(1)}, u32[]{:S(2)}, u32[]{:S(2)}) %collective-permute-start.16) | collective-permute-done | bytes 114720 | tf_op jit(solution)/shard_map/ppermute | solution.py:19
  104.5 2.1 %collective-permute-start.17 = (bf16[8,3584]{1,0:T(8,128)(2,1)S(1)}, bf16[8,3584]{1,0:T(8,128)(2,1)S(1)}, u32[]{:S(2)}, u32[]{:S(2)}) collective-permute-start(bf16[8,3584]{1,0:T(8,128)(2,1)S(1)} %broadcast_select_fusion.4), channel_id=1, source_target_pairs={{0,1},{1,0},{2,3},{3,2},{4,5},{5,4},{6,7},{7,6},{8,9},{9,8},{10,11... | collective-permute-start | bytes 172040 | tf_op jit(solution)/shard_map/ppermute | solution.py:19
  107.4 5.7 %attention.1 = bf16[512,512]{1,0:T(8,128)(2,1)} custom-call(s32[2]{0:T(128)} %pad_add_fusion.where_ref, s32[16,16]{1,0:T(8,128)} %parents_ref.1, s32[16]{0:T(128)} %length_ref.1, bf16[512,576]{1,0:T(8,128)(2,1)} %bitcast.15, bf16[576,512]{1,0:T(8,128)(2,1)} %bitcast.16, bf16[576,512]{1,0:T(8,128)(2,1)} %copy-done.2, bf16[8,576]{1,0:T(8,128)(2,1)} %fresh_ref.1, ...), custom_call_target="tpu_custom_call" | custom-call | flops 1158676480 | bytes 3145728 | tf_op jit(solution)/shard_map/attention/pallas_call | solution.py:122
  (46 shorter events, 7.7 us)
Async XLA Ops:
  2.4 1.8 %collective-permute-start.2 = (bf16[8,3712]{1,0:T(8,128)(2,1)}, bf16[8,3712]{1,0:T(8,128)(2,1)S(1)}, u32[]{:S(2)}, u32[]{:S(2)}) collective-permute-start(bf16[8,3712]{1,0:T(8,128)(2,1)} %get-tuple-element.9), channel_id=1, source_target_pairs={{0,1},{1,0},{2,3},{3,2},{4,5},{5,4},{6,7},{7,6},{8,9},{9,8},{10,11... | collective-permute-start | bytes 178184 | tf_op jit(solution)/shard_map/ppermute | solution.py:19
  5.1 4.5 %collective-permute-start.3 = (bf16[16,3712]{1,0:T(8,128)(2,1)S(1)}, bf16[16,3712]{1,0:T(8,128)(2,1)S(1)}, u32[]{:S(2)}, u32[]{:S(2)}) collective-permute-start(bf16[16,3712]{1,0:T(8,128)(2,1)S(1)} %pad_maximum_fusion), channel_id=1, source_target_pairs={{0,4},{1,5},{2,6},{3,7},{4,0},{5,1},{6,2},{7,3},{8,12},{9,13},{10,... | collective-permute-start | bytes 356360 | tf_op jit(solution)/shard_map/ppermute | solution.py:19
  5.3 7.8 %collective-permute-start.4 = (bf16[16,3712]{1,0:T(8,128)(2,1)S(1)}, bf16[16,3712]{1,0:T(8,128)(2,1)S(1)}, u32[]{:S(2)}, u32[]{:S(2)}) collective-permute-start(bf16[16,3712]{1,0:T(8,128)(2,1)S(1)} %pad_maximum_fusion), channel_id=1, source_target_pairs={{0,8},{1,9},{2,10},{3,11},{4,12},{5,13},{6,14},{7,15},{8,0},{9,1},... | collective-permute-start | bytes 356360 | tf_op jit(solution)/shard_map/ppermute | solution.py:19
  7.6 10.6 %collective-permute-start.5 = (bf16[16,3712]{1,0:T(8,128)(2,1)S(1)}, bf16[16,3712]{1,0:T(8,128)(2,1)S(1)}, u32[]{:S(2)}, u32[]{:S(2)}) collective-permute-start(bf16[16,3712]{1,0:T(8,128)(2,1)S(1)} %pad_maximum_fusion), channel_id=1, source_target_pairs={{0,12},{1,13},{2,14},{3,15},{4,8},{5,9},{6,10},{7,11},{8,4},{9,5},... | collective-permute-start | bytes 356360 | tf_op jit(solution)/shard_map/ppermute | solution.py:19
  18.2 7.9 %collective-permute-start.6 = (bf16[64,3712]{1,0:T(8,128)(2,1)S(1)}, bf16[64,3712]{1,0:T(8,128)(2,1)S(1)}, u32[]{:S(2)}, u32[]{:S(2)}) collective-permute-start(bf16[64,3712]{1,0:T(8,128)(2,1)S(1)} %get-tuple-element.23), channel_id=1, source_target_pairs={{0,2},{1,17},{2,0},{3,19},{4,6},{5,21},{6,4},{7,23},{8,10},{9,25},... | collective-permute-start | bytes 1425416 | tf_op jit(solution)/shard_map/ppermute | solution.py:19
  26.1 13.0 %collective-permute-start.7 = (bf16[128,3712]{1,0:T(8,128)(2,1)S(1)}, bf16[128,3712]{1,0:T(8,128)(2,1)S(1)}, u32[]{:S(2)}, u32[]{:S(2)}) collective-permute-start(bf16[128,3712]{1,0:T(8,128)(2,1)S(1)} %constant_dynamic-update-slice_fusion.5.mine_lo.side_lo), channel_id=1, source_target_pairs={{0,16},{1,3},{2,18},{3,1},{4,20},{5,7},{6,22},{7,5},{8,24},{9,11},... | collective-permute-start | bytes 2850824 | tf_op jit(solution)/shard_map/ppermute | solution.py:19
  26.5 15.9 %collective-permute-start.8 = (bf16[128,3712]{1,0:T(8,128)(2,1)S(1)}, bf16[128,3712]{1,0:T(8,128)(2,1)S(1)}, u32[]{:S(2)}, u32[]{:S(2)}) collective-permute-start(bf16[128,3712]{1,0:T(8,128)(2,1)S(1)} %constant_dynamic-update-slice_fusion.5.mine_lo.side_lo), channel_id=1, source_target_pairs={{0,1},{1,0},{2,3},{3,2},{4,5},{5,4},{6,7},{7,6},{8,9},{9,8},{10,11... | collective-permute-start | bytes 2850824 | tf_op jit(solution)/shard_map/ppermute | solution.py:19
  39.1 5.3 %collective-permute-start.9 = (bf16[128,3712]{1,0:T(8,128)(2,1)S(1)}, bf16[128,3712]{1,0:T(8,128)(2,1)S(1)}, u32[]{:S(2)}, u32[]{:S(2)}) collective-permute-start(bf16[128,3712]{1,0:T(8,128)(2,1)S(1)} %collective-permute-done.7.mine_hi.side_hi), channel_id=1, source_target_pairs={{0,1},{1,0},{2,3},{3,2},{4,5},{5,4},{6,7},{7,6},{8,9},{9,8},{10,11... | collective-permute-start | bytes 2850824 | tf_op jit(solution)/shard_map/ppermute | solution.py:19
  58.6 5.2 %copy-start = (bf16[1,1024,7168]{2,1,0:T(8,128)(2,1)S(1)}, bf16[1,1024,7168]{2,1,0:T(8,128)(2,1)}, u32[]{:S(2)}) copy-start(bf16[1,1024,7168]{2,1,0:T(8,128)(2,1)} %param.21) | copy-start | bytes 44040196
  67.3 27.7 %copy-start.1 = (bf16[1,512,576]{1,2,0:T(8,128)(2,1)S(1)}, bf16[1,512,576]{1,2,0:T(8,128)(2,1)}, u32[]{:S(2)}) copy-start(bf16[1,512,576]{1,2,0:T(8,128)(2,1)} %param.12) | copy-start | bytes 1769476
  67.3 30.6 %copy-start.3 = (bf16[8,576]{1,0:T(8,128)(2,1)S(1)}, bf16[8,576]{1,0:T(8,128)(2,1)}, u32[]{:S(2)}) copy-start(bf16[8,576]{1,0:T(8,128)(2,1)} %fresh_ref.1) | copy-start | bytes 27652
  67.3 4.0 %collective-permute-start.11 = (bf16[128,3584]{1,0:T(8,128)(2,1)S(1)}, bf16[128,3584]{1,0:T(8,128)(2,1)S(1)}, u32[]{:S(2)}, u32[]{:S(2)}) collective-permute-start(bf16[128,3584]{1,0:T(8,128)(2,1)S(1)} %get-tuple-element.13), channel_id=1, source_target_pairs={{0,1},{1,0},{2,3},{3,2},{4,5},{5,4},{6,7},{7,6},{8,9},{9,8},{10,11... | collective-permute-start | bytes 2752520 | tf_op jit(solution)/shard_map/ppermute | solution.py:19
  67.7 4.1 %collective-permute-start.10 = (bf16[128,3584]{1,0:T(8,128)(2,1)S(1)}, bf16[128,3584]{1,0:T(8,128)(2,1)S(1)}, u32[]{:S(2)}, u32[]{:S(2)}) collective-permute-start(bf16[128,3584]{1,0:T(8,128)(2,1)S(1)} %get-tuple-element.11), channel_id=1, source_target_pairs={{0,1},{1,0},{2,3},{3,2},{4,5},{5,4},{6,7},{7,6},{8,9},{9,8},{10,11... | collective-permute-start | bytes 2752520 | tf_op jit(solution)/shard_map/ppermute | solution.py:19
  71.5 12.6 %collective-permute-start.12 = (bf16[128,3584]{1,0:T(8,128)(2,1)S(1)}, bf16[128,3584]{1,0:T(8,128)(2,1)S(1)}, u32[]{:S(2)}, u32[]{:S(2)}) collective-permute-start(bf16[128,3584]{1,0:T(8,128)(2,1)S(1)} %add_convert_fusion), channel_id=1, source_target_pairs={{0,16},{1,3},{2,18},{3,1},{4,20},{5,7},{6,22},{7,5},{8,24},{9,11},... | collective-permute-start | bytes 2752520 | tf_op jit(solution)/shard_map/ppermute | solution.py:19
  84.3 7.7 %collective-permute-start.13 = (bf16[64,3584]{1,0:T(8,128)(2,1)S(1)}, bf16[64,3584]{1,0:T(8,128)(2,1)S(1)}, u32[]{:S(2)}, u32[]{:S(2)}) collective-permute-start(bf16[64,3584]{1,0:T(8,128)(2,1)S(1)} %add_convert_fusion.2), channel_id=1, source_target_pairs={{0,2},{1,17},{2,0},{3,19},{4,6},{5,21},{6,4},{7,23},{8,10},{9,25},... | collective-permute-start | bytes 1376264 | tf_op jit(solution)/shard_map/ppermute | solution.py:19
  92.2 6.4 %collective-permute-start.14 = (bf16[16,3584]{1,0:T(8,128)(2,1)S(1)}, bf16[16,3584]{1,0:T(8,128)(2,1)S(1)}, u32[]{:S(2)}, u32[]{:S(2)}) collective-permute-start(bf16[16,3584]{1,0:T(8,128)(2,1)S(1)} %get-tuple-element.18), channel_id=1, source_target_pairs={{0,4},{1,5},{2,6},{3,7},{4,0},{5,1},{6,2},{7,3},{8,12},{9,13},{10,... | collective-permute-start | bytes 344072 | tf_op jit(solution)/shard_map/ppermute | solution.py:19
  92.3 9.3 %collective-permute-start.15 = (bf16[16,3584]{1,0:T(8,128)(2,1)S(1)}, bf16[16,3584]{1,0:T(8,128)(2,1)S(1)}, u32[]{:S(2)}, u32[]{:S(2)}) collective-permute-start(bf16[16,3584]{1,0:T(8,128)(2,1)S(1)} %get-tuple-element.20), channel_id=1, source_target_pairs={{0,8},{1,9},{2,10},{3,11},{4,12},{5,13},{6,14},{7,15},{8,0},{9,1},... | collective-permute-start | bytes 344072 | tf_op jit(solution)/shard_map/ppermute | solution.py:19
  94.8 9.6 %collective-permute-start.16 = (bf16[16,3584]{1,0:T(8,128)(2,1)S(1)}, bf16[16,3584]{1,0:T(8,128)(2,1)S(1)}, u32[]{:S(2)}, u32[]{:S(2)}) collective-permute-start(bf16[16,3584]{1,0:T(8,128)(2,1)S(1)} %get-tuple-element.19), channel_id=1, source_target_pairs={{0,12},{1,13},{2,14},{3,15},{4,8},{5,9},{6,10},{7,11},{8,4},{9,5},... | collective-permute-start | bytes 344072 | tf_op jit(solution)/shard_map/ppermute | solution.py:19
  95.0 11.6 %collective-permute-start = (bf16[576,512]{1,0:T(8,128)(2,1)S(1)}, bf16[576,512]{1,0:T(8,128)(2,1)S(1)}, u32[]{:S(2)}, u32[]{:S(2)}) collective-permute-start(bf16[576,512]{1,0:T(8,128)(2,1)S(1)} %bitcast.17), channel_id=1, source_target_pairs={{0,1},{1,0},{2,3},{3,2},{4,5},{5,4},{6,7},{7,6},{8,9},{9,8},{10,11... | collective-permute-start | bytes 1769480 | tf_op jit(solution)/shard_map/ppermute | solution.py:19
  97.9 8.7 %collective-permute-start.1 = (bf16[8,576]{1,0:T(8,128)(2,1)S(1)}, bf16[8,576]{1,0:T(8,128)(2,1)S(1)}, u32[]{:S(2)}, u32[]{:S(2)}) collective-permute-start(bf16[8,576]{1,0:T(8,128)(2,1)S(1)} %copy-done.3), channel_id=1, source_target_pairs={{0,1},{1,0},{2,3},{3,2},{4,5},{5,4},{6,7},{7,6},{8,9},{9,8},{10,11... | collective-permute-start | bytes 27656 | tf_op jit(solution)/shard_map/ppermute | solution.py:19
  104.5 8.6 %collective-permute-start.17 = (bf16[8,3584]{1,0:T(8,128)(2,1)S(1)}, bf16[8,3584]{1,0:T(8,128)(2,1)S(1)}, u32[]{:S(2)}, u32[]{:S(2)}) collective-permute-start(bf16[8,3584]{1,0:T(8,128)(2,1)S(1)} %broadcast_select_fusion.4), channel_id=1, source_target_pairs={{0,1},{1,0},{2,3},{3,2},{4,5},{5,4},{6,7},{7,6},{8,9},{9,8},{10,11... | collective-permute-start | bytes 172040 | tf_op jit(solution)/shard_map/ppermute | solution.py:19
  106.6 0.6 copy-start.4
  106.6 0.8 copy-start.2

commit v2 on v1

v2 whole, which is shorter than its diff:
```python
import functools

import jax
import jax.numpy as jnp
from jax import lax
from jax.experimental import pallas as pl
from jax.experimental.pallas import tpu as pltpu
from jax.sharding import PartitionSpec as P


VDIM = 512
AXES = ("req", "ep")
NEG = -1e30
OUT_CHUNKS = 2
BACK_CHUNKS = 2
AHEAD = 3
KERNEL_VMEM = 42 * 1024 * 1024
DOWN_VMEM = 16 * 1024 * 1024

score_scale = 192.0 ** (-0.5)
route_scale = 2.5


def swap(block, count, partner):
    return lax.ppermute(block, AXES, [(i, partner(i)) for i in range(count)])


VMEM = pl.BlockSpec(memory_space=pltpu.VMEM)
SMEM = pl.BlockSpec(memory_space=pltpu.SMEM)
HBM = pl.BlockSpec(memory_space=pltpu.HBM)


def pack_kernel(ep_count, tokens_ref, ids_ref, scores_ref, out_ref):
    width = tokens_ref.shape[1]
    extra = out_ref.shape[1] - width
    scores = scores_ref[...]
    weight = route_scale * scores / jnp.sum(scores, axis=1, keepdims=True)
    ids = ids_ref[...]
    lane = lax.broadcasted_iota(jnp.int32, (ids.shape[0], extra), 1)
    expert = jnp.where(lane >= ep_count, lane - ep_count, lane)
    dense = jnp.zeros(lane.shape, jnp.float32)
    for k in range(ids.shape[1]):
        dense = dense + jnp.where(ids[:, k : k + 1] == expert, weight[:, k : k + 1], 0.0)
    high = dense.astype(jnp.bfloat16).astype(jnp.float32)
    packed = jnp.where(lane < ep_count, high, jnp.where(lane < 2 * ep_count, dense - high, 0.0))
    out_ref[:, :width] = tokens_ref[...]
    out_ref[:, width:] = packed.astype(jnp.bfloat16)


def pack(tokens, route_ids, route_scores, ep_count, extra, chunk, width):
    rows = tokens.shape[0]
    return pl.pallas_call(
        functools.partial(pack_kernel, ep_count),
        grid=(1,),
        in_specs=[
            pl.BlockSpec((rows, width), lambda i: (0, chunk)),
            pl.BlockSpec(route_ids.shape, lambda i: (0, 0)),
            pl.BlockSpec(route_scores.shape, lambda i: (0, 0)),
        ],
        out_specs=pl.BlockSpec((rows, width + extra), lambda i: (0, 0)),
        out_shape=jax.ShapeDtypeStruct((rows, width + extra), jnp.bfloat16),
        name="pack",
    )(tokens, route_ids, route_scores)


def attention_kernel(
    where_ref, parents_ref, length_ref, q_ref, own_ref, other_ref, fresh_ref, other_fresh_ref, out_ref, line_ref
):
    half_index, request = where_ref[0], where_ref[1]
    nodes = line_ref.shape[0]
    tok_dev = nodes // 2
    rows = q_ref.shape[0]
    heads = rows // (tok_dev // pl.num_programs(0))
    length = length_ref[request]
    line_ref[0] = 1
    for node in range(1, nodes):
        line_ref[node] = (1 << node) | line_ref[parents_ref[request, node]]
    span = own_ref.shape[1]
    queries = q_ref[...]
    column = lax.broadcasted_iota(jnp.int32, (1, span), 1)
    dims = (((1,), (0,)), ((), ()))
    flipped = (((1,), (1,)), ((), ()))

    def masked(keys_ref, start):
        scores = lax.dot_general(queries, keys_ref[...], dims, preferred_element_type=jnp.float32) * score_scale
        return jnp.where(column + start < length, scores, NEG)

    scores_own = masked(own_ref, half_index * span)
    scores_other = masked(other_ref, (1 - half_index) * span)

    def tree(keys_ref, first_key):
        scores = lax.dot_general(queries, keys_ref[...], flipped, preferred_element_type=jnp.float32) * score_scale
        key = first_key + lax.broadcasted_iota(jnp.int32, (heads, tok_dev), 1)
        pieces = []
        for t in range(rows // heads):
            node = half_index * tok_dev + pl.program_id(0) * (rows // heads) + t
            ancestors = line_ref[node]
            pieces.append(
                jnp.where((jnp.full(key.shape, ancestors, jnp.int32) >> key) & 1 == 1, scores[t * heads : (t + 1) * heads], NEG)
            )
        return jnp.concatenate(pieces, axis=0)

    scores_fresh = tree(fresh_ref, half_index * tok_dev)
    scores_fresh_other = tree(other_fresh_ref, (1 - half_index) * tok_dev)
    parts = (scores_own, scores_other, scores_fresh, scores_fresh_other)
    top = functools.reduce(jnp.maximum, [jnp.max(part, axis=1, keepdims=True) for part in parts])
    weights = [jnp.exp(part - top) for part in parts]
    total = functools.reduce(jnp.add, [jnp.sum(part, axis=1, keepdims=True) for part in weights])
    vdim = out_ref.shape[1]
    out = lax.dot_general(
        weights[0].astype(jnp.bfloat16), own_ref[:vdim, :], flipped, preferred_element_type=jnp.float32
    )
    out += lax.dot_general(
        weights[1].astype(jnp.bfloat16), other_ref[:vdim, :], flipped, preferred_element_type=jnp.float32
    )
    out += lax.dot_general(
        weights[2].astype(jnp.bfloat16), fresh_ref[:, :vdim], dims, preferred_element_type=jnp.float32
    )
    out += lax.dot_general(
        weights[3].astype(jnp.bfloat16), other_fresh_ref[:, :vdim], dims, preferred_element_type=jnp.float32
    )
    out_ref[...] = (out / total).astype(out_ref.dtype)


def attention(queries, own, other, fresh, other_fresh, parents, cache_len, half_index, request):
    tok_dev, heads, width = queries.shape
    rows = tok_dev * heads
    steps = 2
    whole = lambda array: pl.BlockSpec(array.shape, lambda i, *_: (0,) * array.ndim)
    out = pl.pallas_call(
        attention_kernel,
        out_shape=jax.ShapeDtypeStruct((rows, VDIM), jnp.bfloat16),
        grid_spec=pltpu.PrefetchScalarGridSpec(
            num_scalar_prefetch=3,
            grid=(steps,),
            in_specs=[
                pl.BlockSpec((rows // steps, width), lambda i, *_: (i, 0)),
                whole(own),
                whole(other),
                whole(fresh),
                whole(other_fresh),
            ],
            out_specs=pl.BlockSpec((rows // steps, VDIM), lambda i, *_: (i, 0)),
            scratch_shapes=[pltpu.SMEM((parents.shape[1],), jnp.int32)],
        ),
        cost_estimate=pl.CostEstimate(
            flops=2 * rows * 1040 * (width + VDIM), bytes_accessed=3 * 1024 * 1024, transcendentals=rows * 1040
        ),
        name="attention",
    )(
        jnp.stack([half_index, request]).astype(jnp.int32),
        parents,
        cache_len,
        queries.reshape(rows, width),
        own,
        other,
        fresh,
        other_fresh,
    )
    return out.reshape(tok_dev, heads, VDIM)


def gate_up_kernel(chunk, width, ep_count, tile, *refs):
    place_ref, low_ref, high_ref, other_low_ref, other_high_ref, gate_hbm, up_hbm = refs[:7]
    slots, sems = refs[-2:]
    sums, outs = refs[7:-3] if ep_count else refs[7:-4], refs[-3:-2] if ep_count else refs[-4:-2]
    core = place_ref[0]
    rows = low_ref.shape[0]
    quarter = rows // 2
    starts = ((2 * chunk + core) * width, (2 * chunk + 1 - core) * width)
    order = [(side, i, k) for side in range(2) for i in range(2) for k in range(0, width, tile)]

    def fetch(n):
        side, i, k = order[n]
        source = (gate_hbm, up_hbm)[i]
        at = pl.ds(pl.multiple_of(starts[side] + k, 128), tile)
        return pltpu.make_async_copy(source.at[at, :], slots.at[n], sems.at[n])

    for n in range(min(AHEAD, len(order))):
        fetch(n).start()
    values = [None, None]
    for n, (side, i, k) in enumerate(order):
        if n + AHEAD < len(order):
            fetch(n + AHEAD).start()
        if side == 0:
            pieces = [low_ref[:, k : k + tile], high_ref[:, k : k + tile]]
        else:
            pieces = [
                other_low_ref[:quarter, k : k + tile],
                other_high_ref[:quarter, k : k + tile],
                other_low_ref[quarter:, k : k + tile],
                other_high_ref[quarter:, k : k + tile],
            ]
        fetch(n).wait()
        if quarter < 256:
            pieces = [jnp.concatenate(pieces, axis=0)]
        value = jnp.concatenate(
            [jnp.dot(piece, slots[n], preferred_element_type=jnp.float32) for piece in pieces], axis=0
        )
        if values[i] is None:
            values[i] = value + sums[i][...] if sums else value
        else:
            values[i] += value
    if not ep_count:
        outs[0][...], outs[1][...] = values
        return
    expert = place_ref[1]
    out_ref = outs[0]
    for start, side in ((0, low_ref), (rows, high_ref)):
        beside = side[:, width:].astype(jnp.float32)
        lane = lax.broadcasted_iota(jnp.int32, beside.shape, 1)
        hit = (lane == expert) | (lane == expert + ep_count)
        weight = jnp.sum(jnp.where(hit, beside, 0.0), axis=1, keepdims=True)
        gate = values[0][start : start + rows]
        up = values[1][start : start + rows]
        out_ref[start : start + rows, :] = (gate / (1.0 + jnp.exp(-gate)) * up * weight).astype(out_ref.dtype)


def gate_up(place, chunk, width, low, high, other_low, other_high, w_gate, w_up, sums, ep_count):
    rows, hidden = 2 * low.shape[0], w_gate.shape[1]
    total = jax.ShapeDtypeStruct((rows, hidden), jnp.float32)
    out_shape = jax.ShapeDtypeStruct((rows, hidden), jnp.bfloat16) if ep_count else (total, total)
    tile = width // 2 if width % 256 == 0 else width
    tiles = 4 * width // tile
    return pl.pallas_call(
        functools.partial(gate_up_kernel, chunk, width, ep_count, tile),
        out_shape=out_shape,
        in_specs=[SMEM] + [VMEM] * 4 + [HBM] * 2 + [VMEM] * len(sums),
        out_specs=VMEM if ep_count else (VMEM, VMEM),
        scratch_shapes=[pltpu.VMEM((tiles, tile, hidden), w_gate.dtype), pltpu.SemaphoreType.DMA((tiles,))],
        compiler_params=pltpu.CompilerParams(vmem_limit_bytes=KERNEL_VMEM),
        cost_estimate=pl.CostEstimate(
            flops=8 * rows * width * hidden, bytes_accessed=8 * width * hidden, transcendentals=0
        ),
    )(place, low, high, other_low, other_high, w_gate, w_up, *sums)


def down_kernel(chunk, theirs, place_ref, hidden_ref, weight_ref, low_ref, high_ref):
    core = place_ref[0]
    rows, width = low_ref.shape
    quarter = rows // 2
    side = 1 - core if theirs else core
    at = pl.ds(pl.multiple_of(side * (weight_ref.shape[1] // 2) + chunk * width, 128), width)
    out = jnp.dot(hidden_ref[...], weight_ref[:, at], preferred_element_type=jnp.float32).astype(low_ref.dtype)
    if theirs:
        low_ref[:quarter, :] = out[:quarter]
        low_ref[quarter:, :] = out[rows : rows + quarter]
        high_ref[:quarter, :] = out[quarter:rows]
        high_ref[quarter:, :] = out[rows + quarter :]
    else:
        low_ref[...] = out[:rows]
        high_ref[...] = out[rows:]


def down(place, chunk, width, hidden, w_down, theirs):
    rows, depth = hidden.shape
    out = jax.ShapeDtypeStruct((rows // 2, width), jnp.bfloat16)
    return pl.pallas_call(
        functools.partial(down_kernel, chunk, theirs),
        out_shape=(out, out),
        in_specs=[SMEM, VMEM, VMEM],
        out_specs=(VMEM, VMEM),
        compiler_params=pltpu.CompilerParams(vmem_limit_bytes=DOWN_VMEM),
        cost_estimate=pl.CostEstimate(
            flops=2 * rows * depth * width, bytes_accessed=2 * depth * width, transcendentals=0
        ),
    )(place, hidden, w_down)


def body(
    queries,
    latent_cache,
    new_latents,
    parents,
    cache_len,
    tokens,
    route_ids,
    route_scores,
    w_gate,
    w_up,
    w_down,
):
    ep_count = lax.axis_size("ep")
    count = lax.axis_size("req") * ep_count
    bits = count.bit_length() - 1
    assert count == 1 << bits and bits >= 4
    expert = lax.axis_index("ep")
    position = lax.axis_index("req") * ep_count + expert
    core = position % 2
    even = core == 0
    first, last = 2, 1 << (bits - 1)
    group = 1 << (bits - 3)

    def trade_pair(block):
        return swap(block, count, lambda i: i ^ 1)

    def trade_near(block):
        return swap(block, count, lambda i: i ^ (first if i % 2 == 0 else last))

    def trade_far(block):
        return swap(block, count, lambda i: i ^ (last if i % 2 == 0 else first))

    def trade_group(block, offset):
        return swap(block, count, lambda i: i ^ (offset * 4))

    full = tokens.shape[1]
    half = full // 2
    extra = -(-2 * ep_count // 128) * 128
    place = jnp.stack([core, expert]).astype(jnp.int32)
    tok_dev = tokens.shape[0]

    chunks = OUT_CHUNKS
    width = half // chunks

    def pick(block, own, span):
        part = jnp.where(even == own, block[:, :span], block[:, span : 2 * span])
        return part if block.shape[1] == 2 * span else jnp.concatenate([part, block[:, 2 * span :]], axis=1)

    lows, highs, other_lows, other_highs = [], [], [], []
    line = None

    def finish_near(line):
        low = jnp.concatenate([line, trade_near(line)], axis=0)
        high = trade_far(low)
        lows.append(low)
        highs.append(high)
        other_lows.append(trade_pair(low[:, :width]))
        other_highs.append(trade_pair(high[:, :width]))

    for j in range(chunks):
        if j == chunks - 1:
            block = pack(tokens, route_ids, route_scores, ep_count, extra, j, 2 * width)
        else:
            block = tokens[:, 2 * width * j : 2 * width * (j + 1)]
        rows_of = {k: trade_group(block, k) for k in order_of(group)}
        rows_of[0] = block
        if line is not None:
            rows_of, line = lax.optimization_barrier((rows_of, line))
            finish_near(line)
        stack = jnp.concatenate([rows_of[k] for k in range(group)], axis=0)
        mine, got = pick(stack, True, width), trade_pair(pick(stack, False, width))
        line = jnp.concatenate([jnp.where(even, mine, got), jnp.where(even, got, mine)], axis=0)
    finish_near(line)

    cache = jnp.swapaxes(latent_cache[0], 0, 1)
    other_cache, other_fresh = trade_pair(cache), trade_pair(new_latents)
    attention_out = attention(
        queries, cache, other_cache, new_latents, other_fresh, parents, cache_len, core, position // 2
    )

    sums = ()
    for j in range(chunks):
        sums = gate_up(
            place, j, width, lows[j], highs[j], other_lows[j], other_highs[j], w_gate[0], w_up[0], sums,
            ep_count if j == chunks - 1 else 0,
        )
    hidden = sums

    def rounded(*blocks):
        return functools.reduce(jnp.add, [block.astype(jnp.float32) for block in blocks]).astype(jnp.bfloat16)

    chunks = BACK_CHUNKS
    width = half // chunks
    outs = []
    for j in range(chunks):
        send_low, send_high = down(place, j, width, hidden, w_down[0], True)
        back_high, back_low = trade_pair(send_high), trade_pair(send_low)
        keep_low, keep_high = down(place, j, width, hidden, w_down[0], False)
        far = trade_far(rounded(keep_high, back_high))
        quarter = keep_low.shape[0] // 2
        near = trade_near(rounded(keep_low[quarter:], back_low[quarter:], far[quarter:]))
        line = rounded(keep_low[:quarter], back_low[:quarter], far[:quarter], near)
        first_rows, second_rows = line[: quarter // 2], line[quarter // 2 :]
        keep = jnp.where(even, first_rows, second_rows)
        given = trade_pair(jnp.where(even, second_rows, first_rows))
        whole = jnp.concatenate([jnp.where(even, keep, given), jnp.where(even, given, keep)], axis=1)
        parts = [whole[k * tok_dev : (k + 1) * tok_dev] for k in range(group)]
        moved = {k: trade_group(parts[k], k) for k in order_of(group)}
        outs.append(rounded(parts[0], *[moved[k] for k in range(1, group)]))
    moe_out = jnp.concatenate([out[:, :width] for out in outs] + [out[:, width:] for out in outs], axis=1)
    return (attention_out, moe_out)


def order_of(group):
    return [k for k in range(2, group)] + [1]


def solution(mesh):
    placed = (
        P(("req", "ep"), None, None),
        P(("req", "ep"), None, None),
        P(("req", "ep"), None),
        P(),
        P(),
        P(("req", "ep"), None),
        P(("req", "ep"), None),
        P(("req", "ep"), None),
        P("ep", None, "req"),
        P("ep", None, "req"),
        P("ep", "req", None),
    )
    return jax.shard_map(
        body,
        mesh=mesh,
        in_specs=placed,
        out_specs=(P(("req", "ep"), None, None), P(("req", "ep"), None)),
        check_vma=False,
    )
```

time: 115 us -> 124 us (1.078)
  the two profiles are of different devices: /device:TPU:11 before, /device:TPU:0 now
where the time goes in v2:
time: 124 us; the launch traced here: 123 us
  waiting for transfers between devices  46.4 us (37%)
  Pallas kernels  31.7 us (26%)
  starting transfers between devices  31.3 us (25%)
  local copies, waits for them, and re-layouts  9.61 us (8%)
  other arithmetic  3.3 us (3%)
    ppermute x34, waiting for transfers between devices, swap(): return lax.ppermute(block, AXES, [(i, partner(i)) for i in range(count)])  46.4 us
    ppermute x34, starting transfers between devices, swap(): return lax.ppermute(block, AXES, [(i, partner(i)) for i in range(count)])  31.3 us
    pallas_call x2, Pallas kernels, gate_up(): pl.pallas_call(functools.partial(gate_up_kernel, chunk, width, ep_count,...  17.4 us
    unnamed x22, local copies, waits for them, and re-layouts  8.67 us
    pallas_call x4, Pallas kernels, down(): pl.pallas_call(functools.partial(down_kernel, chunk, theirs), out_shape=(...  6.73 us
    pallas_call x1, Pallas kernels, attention(): pl.pallas_call(attention_kernel, out_shape=jax.ShapeDtypeStruct((rows, VD...  5.87 us
  transfers between devices with their start and end apart: 34, of which 15 were waited for; matrix products, arithmetic and copies ran while one was open for 2% of the time, Pallas kernels for 26%

profile of v2, /device:TPU:0, one launch (start us, length us, event | category | flops | bytes accessed | tf_op | source)
XLA Modules:
  0.0 123.3 jit_solution(15068606532274526431)
XLA Ops:
  1.5 3.1 %collective-permute-start.5 = (bf16[8,3584]{1,0:T(8,128)(2,1)S(1)}, bf16[8,3584]{1,0:T(8,128)(2,1)S(1)}, u32[]{:S(2)}, u32[]{:S(2)}) collective-permute-start(bf16[8,3584]{1,0:T(8,128)(2,1)S(1)} %slice.113), channel_id=1, source_target_pairs={{0,4},{1,5},{2,6},{3,7},{4,0},{5,1},{6,2},{7,3},{8,12},{9,13},{10,... | collective-permute-start | bytes 172040 | tf_op jit(solution)/shard_map/ppermute | solution.py:25
  4.5 2.6 %collective-permute-start.6 = (bf16[8,3584]{1,0:T(8,128)(2,1)S(1)}, bf16[8,3584]{1,0:T(8,128)(2,1)S(1)}, u32[]{:S(2)}, u32[]{:S(2)}) collective-permute-start(bf16[8,3584]{1,0:T(8,128)(2,1)S(1)} %slice.113), channel_id=1, source_target_pairs={{0,8},{1,9},{2,10},{3,11},{4,12},{5,13},{6,14},{7,15},{8,0},{9,1},... | collective-permute-start | bytes 172040 | tf_op jit(solution)/shard_map/ppermute | solution.py:25
  7.1 3.6 %collective-permute-done.6 = bf16[8,3584]{1,0:T(8,128)(2,1)S(1)} collective-permute-done((bf16[8,3584]{1,0:T(8,128)(2,1)S(1)}, bf16[8,3584]{1,0:T(8,128)(2,1)S(1)}, u32[]{:S(2)}, u32[]{:S(2)}) %collective-permute-start.6) | collective-permute-done | bytes 57376 | tf_op jit(solution)/shard_map/ppermute | solution.py:25
  10.7 2.4 %collective-permute-done.7 = bf16[8,3584]{1,0:T(8,128)(2,1)S(1)} collective-permute-done((bf16[8,3584]{1,0:T(8,128)(2,1)S(1)}, bf16[8,3584]{1,0:T(8,128)(2,1)S(1)}, u32[]{:S(2)}, u32[]{:S(2)}) %collective-permute-start.7) | collective-permute-done | bytes 57376 | tf_op jit(solution)/shard_map/ppermute | solution.py:25
  14.8 1.8 %collective-permute-start.3 = (bf16[8,3712]{1,0:T(8,128)(2,1)}, bf16[8,3712]{1,0:T(8,128)(2,1)S(1)}, u32[]{:S(2)}, u32[]{:S(2)}) collective-permute-start(bf16[8,3712]{1,0:T(8,128)(2,1)} %pack.1), channel_id=1, source_target_pairs={{0,8},{1,9},{2,10},{3,11},{4,12},{5,13},{6,14},{7,15},{8,0},{9,1},... | collective-permute-start | bytes 178184 | tf_op jit(solution)/shard_map/ppermute | solution.py:25
  16.7 2.6 %collective-permute-start.4 = (bf16[8,3712]{1,0:T(8,128)(2,1)}, bf16[8,3712]{1,0:T(8,128)(2,1)S(1)}, u32[]{:S(2)}, u32[]{:S(2)}) collective-permute-start(bf16[8,3712]{1,0:T(8,128)(2,1)} %pack.1), channel_id=1, source_target_pairs={{0,12},{1,13},{2,14},{3,15},{4,8},{5,9},{6,10},{7,11},{8,4},{9,5},... | collective-permute-start | bytes 178184 | tf_op jit(solution)/shard_map/ppermute | solution.py:25
  20.5 2.7 %collective-permute-done.3 = bf16[8,3712]{1,0:T(8,128)(2,1)S(1)} collective-permute-done((bf16[8,3712]{1,0:T(8,128)(2,1)}, bf16[8,3712]{1,0:T(8,128)(2,1)S(1)}, u32[]{:S(2)}, u32[]{:S(2)}) %collective-permute-start.3) | collective-permute-done | bytes 59424 | tf_op jit(solution)/shard_map/ppermute | solution.py:25
  27.8 2.4 %collective-permute-done.14 = bf16[64,1792]{1,0:T(8,128)(2,1)S(1)} collective-permute-done((bf16[64,1792]{1,0:T(8,128)(2,1)S(1)}, bf16[64,1792]{1,0:T(8,128)(2,1)S(1)}, u32[]{:S(2)}, u32[]{:S(2)}) %collective-permute-start.14) | collective-permute-done | bytes 229408 | tf_op jit(solution)/shard_map/ppermute | solution.py:25
  31.8 3.7 %collective-permute-done.10 = bf16[64,1920]{1,0:T(8,128)(2,1)S(1)} collective-permute-done((bf16[64,1920]{1,0:T(8,128)(2,1)S(1)}, bf16[64,1920]{1,0:T(8,128)(2,1)S(1)}, u32[]{:S(2)}, u32[]{:S(2)}) %collective-permute-start.10) | collective-permute-done | bytes 245792 | tf_op jit(solution)/shard_map/ppermute | solution.py:25
  35.6 1.7 %collective-permute-start.11 = (bf16[128,1920]{1,0:T(8,128)(2,1)S(1)}, bf16[128,1920]{1,0:T(8,128)(2,1)S(1)}, u32[]{:S(2)}, u32[]{:S(2)}) collective-permute-start(bf16[128,1920]{1,0:T(8,128)(2,1)S(1)} %pad_maximum_fusion.refs_1_), channel_id=1, source_target_pairs={{0,16},{1,3},{2,18},{3,1},{4,20},{5,7},{6,22},{7,5},{8,24},{9,11},... | collective-permute-start | bytes 1474568 | tf_op jit(solution)/shard_map/ppermute | solution.py:25
  39.4 5.1 %collective-permute-done.11.refs_2_ = bf16[128,1920]{1,0:T(8,128)(2,1)S(1)} collective-permute-done((bf16[128,1920]{1,0:T(8,128)(2,1)S(1)}, bf16[128,1920]{1,0:T(8,128)(2,1)S(1)}, u32[]{:S(2)}, u32[]{:S(2)}) %collective-permute-start.11) | collective-permute-done | bytes 491552 | tf_op jit(solution)/shard_map/ppermute | solution.py:25
  47.0 8.8 %shard_map.122 = (f32[256,1024]{1,0:T(8,128)S(1)}, f32[256,1024]{1,0:T(8,128)S(1)}) custom-call(s32[2]{0:T(128)S(1)} %pad_add_fusion.1.refs_0_.place_ref, bf16[128,1792]{1,0:T(8,128)(2,1)S(1)} %constant_dynamic-update-slice_fusion.4.refs_1_, bf16[128,1792]{1,0:T(8,128)(2,1)S(1)} %collective-permute-done.15.refs_2_, ...), custom_call_target="tpu_custom_call" | custom-call | flops 3758096384 | bytes 14680064 | tf_op jit(solution)/shard_map/pallas_call | solution.py:225
  55.8 8.7 %shard_map.123.hidden_ref = bf16[256,1024]{1,0:T(8,128)(2,1)S(1)} custom-call(s32[2]{0:T(128)S(1)} %pad_add_fusion.1.refs_0_.place_ref, bf16[128,1920]{1,0:T(8,128)(2,1)S(1)} %pad_maximum_fusion.refs_1_, bf16[128,1920]{1,0:T(8,128)(2,1)S(1)} %collective-permute-done.11.refs_2_, bf16[128,1792]{1,0:T(8,128)(2,1)S(1)} %collective-permute-done.12.refs_3_, ...), custom_call_target="tpu_custom_call" | custom-call | flops 3758096384 | bytes 14680064 | tf_op jit(solution)/shard_map/pallas_call | solution.py:225
  67.7 5.9 %attention.1 = bf16[512,512]{1,0:T(8,128)(2,1)} custom-call(s32[2]{0:T(128)} %pad_add_fusion.where_ref, s32[16,16]{1,0:T(8,128)} %parents_ref.1, s32[16]{0:T(128)} %length_ref.1, bf16[512,576]{1,0:T(8,128)(2,1)} %bitcast.21, bf16[576,512]{1,0:T(8,128)(2,1)} %bitcast.23, bf16[576,512]{1,0:T(8,128)(2,1)} %copy-done.3, bf16[8,576]{1,0:T(8,128)(2,1)} %fresh_ref.1, ...), custom_call_target="tpu_custom_call" | custom-call | flops 1158676480 | bytes 3145728 | tf_op jit(solution)/shard_map/attention/pallas_call | solution.py:130
  74.1 5.2 %copy-done = bf16[1,1024,7168]{2,1,0:T(8,128)(2,1)S(1)} copy-done((bf16[1,1024,7168]{2,1,0:T(8,128)(2,1)S(1)}, bf16[1,1024,7168]{2,1,0:T(8,128)(2,1)}, u32[]{:S(2)}) %copy-start) | copy-done | bytes 14680088
  83.2 1.7 %shard_map.126 = (bf16[128,1792]{1,0:T(8,128)(2,1)S(1)}, bf16[128,1792]{1,0:T(8,128)(2,1)S(1)}) custom-call(s32[2]{0:T(128)S(1)} %pad_add_fusion.1.refs_0_.place_ref, bf16[256,1024]{1,0:T(8,128)(2,1)S(1)} %shard_map.123.hidden_ref, bf16[1024,7168]{1,0:T(8,128)(2,1)S(1)} %bitcast.16), custom_call_target="tpu_custom_call" | custom-call | flops 939524096 | bytes 3670016 | tf_op jit(solution)/shard_map/pallas_call | solution.py:258
  86.0 1.7 %collective-permute-start.20 = (bf16[128,1792]{1,0:T(8,128)(2,1)S(1)}, bf16[128,1792]{1,0:T(8,128)(2,1)S(1)}, u32[]{:S(2)}, u32[]{:S(2)}) collective-permute-start(bf16[128,1792]{1,0:T(8,128)(2,1)S(1)} %add_convert_fusion.1), channel_id=1, source_target_pairs={{0,16},{1,3},{2,18},{3,1},{4,20},{5,7},{6,22},{7,5},{8,24},{9,11},... | collective-permute-start | bytes 1376264 | tf_op jit(solution)/shard_map/ppermute | solution.py:25
  88.3 6.3 %collective-permute-done.20 = bf16[128,1792]{1,0:T(8,128)(2,1)S(1)} collective-permute-done((bf16[128,1792]{1,0:T(8,128)(2,1)S(1)}, bf16[128,1792]{1,0:T(8,128)(2,1)S(1)}, u32[]{:S(2)}, u32[]{:S(2)}) %collective-permute-start.20) | collective-permute-done | bytes 458784 | tf_op jit(solution)/shard_map/ppermute | solution.py:25
  95.7 6.4 %collective-permute-done.28 = bf16[128,1792]{1,0:T(8,128)(2,1)S(1)} collective-permute-done((bf16[128,1792]{1,0:T(8,128)(2,1)S(1)}, bf16[128,1792]{1,0:T(8,128)(2,1)S(1)}, u32[]{:S(2)}, u32[]{:S(2)}) %collective-permute-start.28) | collective-permute-done | bytes 458784 | tf_op jit(solution)/shard_map/ppermute | solution.py:25
  103.5 4.8 %collective-permute-done.29 = bf16[64,1792]{1,0:T(8,128)(2,1)S(1)} collective-permute-done((bf16[64,1792]{1,0:T(8,128)(2,1)S(1)}, bf16[64,1792]{1,0:T(8,128)(2,1)S(1)}, u32[]{:S(2)}, u32[]{:S(2)}) %collective-permute-start.29) | collective-permute-done | bytes 229408 | tf_op jit(solution)/shard_map/ppermute | solution.py:25
  111.3 1.8 %collective-permute-start.25 = (bf16[8,3584]{1,0:T(8,128)(2,1)S(1)}, bf16[8,3584]{1,0:T(8,128)(2,1)S(1)}, u32[]{:S(2)}, u32[]{:S(2)}) collective-permute-start(bf16[8,3584]{1,0:T(8,128)(2,1)S(1)} %get-tuple-element.43), channel_id=1, source_target_pairs={{0,12},{1,13},{2,14},{3,15},{4,8},{5,9},{6,10},{7,11},{8,4},{9,5},... | collective-permute-start | bytes 172040 | tf_op jit(solution)/shard_map/ppermute | solution.py:25
  113.3 2.5 %collective-permute-start.32 = (bf16[8,3584]{1,0:T(8,128)(2,1)S(1)}, bf16[8,3584]{1,0:T(8,128)(2,1)S(1)}, u32[]{:S(2)}, u32[]{:S(2)}) collective-permute-start(bf16[8,3584]{1,0:T(8,128)(2,1)S(1)} %get-tuple-element.47), channel_id=1, source_target_pairs={{0,8},{1,9},{2,10},{3,11},{4,12},{5,13},{6,14},{7,15},{8,0},{9,1},... | collective-permute-start | bytes 172040 | tf_op jit(solution)/shard_map/ppermute | solution.py:25
  115.8 1.8 %collective-permute-start.33 = (bf16[8,3584]{1,0:T(8,128)(2,1)S(1)}, bf16[8,3584]{1,0:T(8,128)(2,1)S(1)}, u32[]{:S(2)}, u32[]{:S(2)}) collective-permute-start(bf16[8,3584]{1,0:T(8,128)(2,1)S(1)} %get-tuple-element.46), channel_id=1, source_target_pairs={{0,12},{1,13},{2,14},{3,15},{4,8},{5,9},{6,10},{7,11},{8,4},{9,5},... | collective-permute-start | bytes 172040 | tf_op jit(solution)/shard_map/ppermute | solution.py:25
  118.5 4.1 %collective-permute-done.32 = bf16[8,3584]{1,0:T(8,128)(2,1)S(1)} collective-permute-done((bf16[8,3584]{1,0:T(8,128)(2,1)S(1)}, bf16[8,3584]{1,0:T(8,128)(2,1)S(1)}, u32[]{:S(2)}, u32[]{:S(2)}) %collective-permute-start.32) | collective-permute-done | bytes 57376 | tf_op jit(solution)/shard_map/ppermute | solution.py:25
  (109 shorter events, 31.2 us)
Async XLA Ops:
  4.5 6.2 %collective-permute-start.6 = (bf16[8,3584]{1,0:T(8,128)(2,1)S(1)}, bf16[8,3584]{1,0:T(8,128)(2,1)S(1)}, u32[]{:S(2)}, u32[]{:S(2)}) collective-permute-start(bf16[8,3584]{1,0:T(8,128)(2,1)S(1)} %slice.113), channel_id=1, source_target_pairs={{0,8},{1,9},{2,10},{3,11},{4,12},{5,13},{6,14},{7,15},{8,0},{9,1},... | collective-permute-start | bytes 172040 | tf_op jit(solution)/shard_map/ppermute | solution.py:25
  14.8 8.4 %collective-permute-start.3 = (bf16[8,3712]{1,0:T(8,128)(2,1)}, bf16[8,3712]{1,0:T(8,128)(2,1)S(1)}, u32[]{:S(2)}, u32[]{:S(2)}) collective-permute-start(bf16[8,3712]{1,0:T(8,128)(2,1)} %pack.1), channel_id=1, source_target_pairs={{0,8},{1,9},{2,10},{3,11},{4,12},{5,13},{6,14},{7,15},{8,0},{9,1},... | collective-permute-start | bytes 178184 | tf_op jit(solution)/shard_map/ppermute | solution.py:25
  16.7 6.5 %collective-permute-start.4 = (bf16[8,3712]{1,0:T(8,128)(2,1)}, bf16[8,3712]{1,0:T(8,128)(2,1)S(1)}, u32[]{:S(2)}, u32[]{:S(2)}) collective-permute-start(bf16[8,3712]{1,0:T(8,128)(2,1)} %pack.1), channel_id=1, source_target_pairs={{0,12},{1,13},{2,14},{3,15},{4,8},{5,9},{6,10},{7,11},{8,4},{9,5},... | collective-permute-start | bytes 178184 | tf_op jit(solution)/shard_map/ppermute | solution.py:25
  27.2 8.4 %collective-permute-start.10 = (bf16[64,1920]{1,0:T(8,128)(2,1)S(1)}, bf16[64,1920]{1,0:T(8,128)(2,1)S(1)}, u32[]{:S(2)}, u32[]{:S(2)}) collective-permute-start(bf16[64,1920]{1,0:T(8,128)(2,1)S(1)} %pad_maximum_fusion.1), channel_id=1, source_target_pairs={{0,2},{1,17},{2,0},{3,19},{4,6},{5,21},{6,4},{7,23},{8,10},{9,25},... | collective-permute-start | bytes 737288 | tf_op jit(solution)/shard_map/ppermute | solution.py:25
  30.2 8.5 %collective-permute-start.15 = (bf16[128,1792]{1,0:T(8,128)(2,1)S(1)}, bf16[128,1792]{1,0:T(8,128)(2,1)S(1)}, u32[]{:S(2)}, u32[]{:S(2)}) collective-permute-start(bf16[128,1792]{1,0:T(8,128)(2,1)S(1)} %constant_dynamic-update-slice_fusion.4.refs_1_), channel_id=1, source_target_pairs={{0,16},{1,3},{2,18},{3,1},{4,20},{5,7},{6,22},{7,5},{8,24},{9,11},... | collective-permute-start | bytes 1376264 | tf_op jit(solution)/shard_map/ppermute | solution.py:25
  35.6 8.9 %collective-permute-start.11 = (bf16[128,1920]{1,0:T(8,128)(2,1)S(1)}, bf16[128,1920]{1,0:T(8,128)(2,1)S(1)}, u32[]{:S(2)}, u32[]{:S(2)}) collective-permute-start(bf16[128,1920]{1,0:T(8,128)(2,1)S(1)} %pad_maximum_fusion.refs_1_), channel_id=1, source_target_pairs={{0,16},{1,3},{2,18},{3,1},{4,20},{5,7},{6,22},{7,5},{8,24},{9,11},... | collective-permute-start | bytes 1474568 | tf_op jit(solution)/shard_map/ppermute | solution.py:25
  37.3 7.4 %collective-permute-start.16 = (bf16[128,1792]{1,0:T(8,128)(2,1)S(1)}, bf16[128,1792]{1,0:T(8,128)(2,1)S(1)}, u32[]{:S(2)}, u32[]{:S(2)}) collective-permute-start(bf16[128,1792]{1,0:T(8,128)(2,1)S(1)} %constant_dynamic-update-slice_fusion.4.refs_1_), channel_id=1, source_target_pairs={{0,1},{1,0},{2,3},{3,2},{4,5},{5,4},{6,7},{7,6},{8,9},{9,8},{10,11... | collective-permute-start | bytes 1376264 | tf_op jit(solution)/shard_map/ppermute | solution.py:25
  38.8 6.4 %collective-permute-start.17 = (bf16[128,1792]{1,0:T(8,128)(2,1)S(1)}, bf16[128,1792]{1,0:T(8,128)(2,1)S(1)}, u32[]{:S(2)}, u32[]{:S(2)}) collective-permute-start(bf16[128,1792]{1,0:T(8,128)(2,1)S(1)} %collective-permute-done.15.refs_2_), channel_id=1, source_target_pairs={{0,1},{1,0},{2,3},{3,2},{4,5},{5,4},{6,7},{7,6},{8,9},{9,8},{10,11... | collective-permute-start | bytes 1376264 | tf_op jit(solution)/shard_map/ppermute | solution.py:25
  38.8 28.1 %collective-permute-start = (bf16[576,512]{1,0:T(8,128)(2,1)}, bf16[576,512]{1,0:T(8,128)(2,1)S(1)}, u32[]{:S(2)}, u32[]{:S(2)}) collective-permute-start(bf16[576,512]{1,0:T(8,128)(2,1)} %bitcast.22), channel_id=1, source_target_pairs={{0,1},{1,0},{2,3},{3,2},{4,5},{5,4},{6,7},{7,6},{8,9},{9,8},{10,11... | collective-permute-start | bytes 1769480 | tf_op jit(solution)/shard_map/ppermute | solution.py:25
  39.3 16.4 %collective-permute-start.12 = (bf16[128,1792]{1,0:T(8,128)(2,1)S(1)}, bf16[128,1792]{1,0:T(8,128)(2,1)S(1)}, u32[]{:S(2)}, u32[]{:S(2)}) collective-permute-start(bf16[128,1792]{1,0:T(8,128)(2,1)S(1)} %slice.154), channel_id=1, source_target_pairs={{0,1},{1,0},{2,3},{3,2},{4,5},{5,4},{6,7},{7,6},{8,9},{9,8},{10,11... | collective-permute-start | bytes 1376264 | tf_op jit(solution)/shard_map/ppermute | solution.py:25
  44.5 11.2 %collective-permute-start.13 = (bf16[128,1792]{1,0:T(8,128)(2,1)S(1)}, bf16[128,1792]{1,0:T(8,128)(2,1)S(1)}, u32[]{:S(2)}, u32[]{:S(2)}) collective-permute-start(bf16[128,1792]{1,0:T(8,128)(2,1)S(1)} %slice.155), channel_id=1, source_target_pairs={{0,1},{1,0},{2,3},{3,2},{4,5},{5,4},{6,7},{7,6},{8,9},{9,8},{10,11... | collective-permute-start | bytes 1376264 | tf_op jit(solution)/shard_map/ppermute | solution.py:25
  44.7 22.2 %collective-permute-start.1 = (bf16[8,576]{1,0:T(8,128)(2,1)}, bf16[8,576]{1,0:T(8,128)(2,1)S(1)}, u32[]{:S(2)}, u32[]{:S(2)}) collective-permute-start(bf16[8,576]{1,0:T(8,128)(2,1)} %fresh_ref.1), channel_id=1, source_target_pairs={{0,1},{1,0},{2,3},{3,2},{4,5},{5,4},{6,7},{7,6},{8,9},{9,8},{10,11... | collective-permute-start | bytes 27656 | tf_op jit(solution)/shard_map/ppermute | solution.py:25
  66.2 18.7 %collective-permute-start.19 = (bf16[128,1792]{1,0:T(8,128)(2,1)S(1)}, bf16[128,1792]{1,0:T(8,128)(2,1)}, u32[]{:S(2)}, u32[]{:S(2)}) collective-permute-start(bf16[128,1792]{1,0:T(8,128)(2,1)S(1)} %get-tuple-element.27), channel_id=1, source_target_pairs={{0,1},{1,0},{2,3},{3,2},{4,5},{5,4},{6,7},{7,6},{8,9},{9,8},{10,11... | collective-permute-start | bytes 1376264 | tf_op jit(solution)/shard_map/ppermute | solution.py:25
  73.6 14.7 %collective-permute-start.18 = (bf16[128,1792]{1,0:T(8,128)(2,1)S(1)}, bf16[128,1792]{1,0:T(8,128)(2,1)S(1)}, u32[]{:S(2)}, u32[]{:S(2)}) collective-permute-start(bf16[128,1792]{1,0:T(8,128)(2,1)S(1)} %get-tuple-element.25), channel_id=1, source_target_pairs={{0,1},{1,0},{2,3},{3,2},{4,5},{5,4},{6,7},{7,6},{8,9},{9,8},{10,11... | collective-permute-start | bytes 1376264 | tf_op jit(solution)/shard_map/ppermute | solution.py:25
  80.9 6.8 %collective-permute-start.27 = (bf16[128,1792]{1,0:T(8,128)(2,1)S(1)}, bf16[128,1792]{1,0:T(8,128)(2,1)S(1)}, u32[]{:S(2)}, u32[]{:S(2)}) collective-permute-start(bf16[128,1792]{1,0:T(8,128)(2,1)S(1)} %get-tuple-element.31), channel_id=1, source_target_pairs={{0,1},{1,0},{2,3},{3,2},{4,5},{5,4},{6,7},{7,6},{8,9},{9,8},{10,11... | collective-permute-start | bytes 1376264 | tf_op jit(solution)/shard_map/ppermute | solution.py:25
  81.0 14.7 %collective-permute-start.26 = (bf16[128,1792]{1,0:T(8,128)(2,1)S(1)}, bf16[128,1792]{1,0:T(8,128)(2,1)S(1)}, u32[]{:S(2)}, u32[]{:S(2)}) collective-permute-start(bf16[128,1792]{1,0:T(8,128)(2,1)S(1)} %get-tuple-element.29), channel_id=1, source_target_pairs={{0,1},{1,0},{2,3},{3,2},{4,5},{5,4},{6,7},{7,6},{8,9},{9,8},{10,11... | collective-permute-start | bytes 1376264 | tf_op jit(solution)/shard_map/ppermute | solution.py:25
  86.0 8.5 %collective-permute-start.20 = (bf16[128,1792]{1,0:T(8,128)(2,1)S(1)}, bf16[128,1792]{1,0:T(8,128)(2,1)S(1)}, u32[]{:S(2)}, u32[]{:S(2)}) collective-permute-start(bf16[128,1792]{1,0:T(8,128)(2,1)S(1)} %add_convert_fusion.1), channel_id=1, source_target_pairs={{0,16},{1,3},{2,18},{3,1},{4,20},{5,7},{6,22},{7,5},{8,24},{9,11},... | collective-permute-start | bytes 1376264 | tf_op jit(solution)/shard_map/ppermute | solution.py:25
  87.8 14.3 %collective-permute-start.28 = (bf16[128,1792]{1,0:T(8,128)(2,1)S(1)}, bf16[128,1792]{1,0:T(8,128)(2,1)S(1)}, u32[]{:S(2)}, u32[]{:S(2)}) collective-permute-start(bf16[128,1792]{1,0:T(8,128)(2,1)S(1)} %add_convert_fusion), channel_id=1, source_target_pairs={{0,16},{1,3},{2,18},{3,1},{4,20},{5,7},{6,22},{7,5},{8,24},{9,11},... | collective-permute-start | bytes 1376264 | tf_op jit(solution)/shard_map/ppermute | solution.py:25
  94.7 8.6 %collective-permute-start.21 = (bf16[64,1792]{1,0:T(8,128)(2,1)S(1)}, bf16[64,1792]{1,0:T(8,128)(2,1)S(1)}, u32[]{:S(2)}, u32[]{:S(2)}) collective-permute-start(bf16[64,1792]{1,0:T(8,128)(2,1)S(1)} %add_convert_fusion.5), channel_id=1, source_target_pairs={{0,2},{1,17},{2,0},{3,19},{4,6},{5,21},{6,4},{7,23},{8,10},{9,25},... | collective-permute-start | bytes 688136 | tf_op jit(solution)/shard_map/ppermute | solution.py:25
  108.6 7.2 %collective-permute-start.23 = (bf16[8,3584]{1,0:T(8,128)(2,1)S(1)}, bf16[8,3584]{1,0:T(8,128)(2,1)S(1)}, u32[]{:S(2)}, u32[]{:S(2)}) collective-permute-start(bf16[8,3584]{1,0:T(8,128)(2,1)S(1)} %get-tuple-element.42), channel_id=1, source_target_pairs={{0,4},{1,5},{2,6},{3,7},{4,0},{5,1},{6,2},{7,3},{8,12},{9,13},{10,... | collective-permute-start | bytes 172040 | tf_op jit(solution)/shard_map/ppermute | solution.py:25
  109.7 8.1 %collective-permute-start.24 = (bf16[8,3584]{1,0:T(8,128)(2,1)S(1)}, bf16[8,3584]{1,0:T(8,128)(2,1)S(1)}, u32[]{:S(2)}, u32[]{:S(2)}) collective-permute-start(bf16[8,3584]{1,0:T(8,128)(2,1)S(1)} %get-tuple-element.44), channel_id=1, source_target_pairs={{0,8},{1,9},{2,10},{3,11},{4,12},{5,13},{6,14},{7,15},{8,0},{9,1},... | collective-permute-start | bytes 172040 | tf_op jit(solution)/shard_map/ppermute | solution.py:25
  111.3 6.6 %collective-permute-start.25 = (bf16[8,3584]{1,0:T(8,128)(2,1)S(1)}, bf16[8,3584]{1,0:T(8,128)(2,1)S(1)}, u32[]{:S(2)}, u32[]{:S(2)}) collective-permute-start(bf16[8,3584]{1,0:T(8,128)(2,1)S(1)} %get-tuple-element.43), channel_id=1, source_target_pairs={{0,12},{1,13},{2,14},{3,15},{4,8},{5,9},{6,10},{7,11},{8,4},{9,5},... | collective-permute-start | bytes 172040 | tf_op jit(solution)/shard_map/ppermute | solution.py:25
  113.3 9.3 %collective-permute-start.32 = (bf16[8,3584]{1,0:T(8,128)(2,1)S(1)}, bf16[8,3584]{1,0:T(8,128)(2,1)S(1)}, u32[]{:S(2)}, u32[]{:S(2)}) collective-permute-start(bf16[8,3584]{1,0:T(8,128)(2,1)S(1)} %get-tuple-element.47), channel_id=1, source_target_pairs={{0,8},{1,9},{2,10},{3,11},{4,12},{5,13},{6,14},{7,15},{8,0},{9,1},... | collective-permute-start | bytes 172040 | tf_op jit(solution)/shard_map/ppermute | solution.py:25
  115.8 6.8 %collective-permute-start.33 = (bf16[8,3584]{1,0:T(8,128)(2,1)S(1)}, bf16[8,3584]{1,0:T(8,128)(2,1)S(1)}, u32[]{:S(2)}, u32[]{:S(2)}) collective-permute-start(bf16[8,3584]{1,0:T(8,128)(2,1)S(1)} %get-tuple-element.46), channel_id=1, source_target_pairs={{0,12},{1,13},{2,14},{3,15},{4,8},{5,9},{6,10},{7,11},{8,4},{9,5},... | collective-permute-start | bytes 172040 | tf_op jit(solution)/shard_map/ppermute | solution.py:25
  (19 other events, 112.9 us)
